TPU v7x, 512 devices: a whole 4x4x16 slice. The times are simulated.
512 devices in a mesh: batch: 64 (over z, y_hi, core), coef: 8 (over y_lo, x).
Axes of the slice: x: 4, y: 4 (y_hi: 2, y_lo: 2; y = y_hi * 2 + y_lo), z: 16, core: 2. Of those that a mesh axis runs over, the one named last changes fastest.
Arguments:
- jac_blocks: bfloat16 [2048, 8, 2, 128, 128], P(('batch', 'coef')), may hold values from -0.52734375 to 0.52734375
- col_blocks: int32 [8, 2048, 2], P('coef', 'batch'), may hold values from 0 to 63, all different within a row; in each aligned block of 32 rows (0 to 31, 32 to 63, ..., all dimensions but the last counted through in order) at most 2 rows name the same one
- residual: float32 [2048, 128], P('batch'), may hold values from -6 to 6
- run_of_half: int32 [4096], P('batch'), may hold values from 0 to 4095, each once
- run_scale: bfloat16 [4096], replicated, may hold values from 0.25 to 4
Outputs:
- diag_blocks: float32 [8, 64, 128, 128], P('coef', 'batch')
- gradient: float32 [8, 64, 128], P('coef', 'batch')
Inputs may be any that keep to these rules, and one draw needn't show every extreme that they name: `col_blocks`: the 2 column blocks of one row block in one group differ. For each group, among the row blocks of one batch index (aligned blocks of the row-block dimension), no column block is named more than 2 times, a bound that some block reaches. `run_of_half`: every run appears exactly once.
All inputs are finite; a program needn't handle non-finite values.
Results may differ from a plain program's by a relative error of at most 0.00043.
Values may be sent and summed in bfloat16 or wider, within the bound.
No kernel may reach another device: no remote copies, remote signals or barrier semaphores. Data moves between devices by JAX's collectives and lax.ppermute only.
A program may use at most 64 MiB of HBM per device.

v0:
```python
import jax
import jax.numpy as jnp
from jax import lax
from jax.sharding import PartitionSpec as P

BS = 128
PAIR = 2


def shards(jac_blocks, col_blocks, residual, run_of_half, run_scale):
    width = lax.axis_size("batch")
    myself = lax.axis_index("batch")
    moved = lax.all_to_all(jac_blocks, "coef", split_axis=1, concat_axis=0, tiled=True)
    items = moved.reshape(-1, BS, BS)
    targets = col_blocks.reshape(-1)
    scale_rows = run_scale.astype(jnp.float32)[run_of_half].reshape(-1, 2)
    weights = jnp.repeat(scale_rows, BS // 2, axis=1)
    item_w = jnp.repeat(weights, PAIR, axis=0)
    item_res = jnp.repeat(residual, PAIR, axis=0)
    onehot = (targets[:, None] == jnp.arange(width, dtype=jnp.int32)[None, :]).astype(jnp.float32)
    gterms = jnp.einsum(
        "iak,ia->ik", items.astype(jnp.float32), item_w * item_res, precision=lax.Precision.HIGHEST
    )
    gpart = jnp.einsum("il,ik->lk", onehot, gterms, precision=lax.Precision.HIGHEST)
    gtotal = lax.psum(gpart, "batch")
    gradient = lax.dynamic_slice_in_dim(gtotal, myself, 1, 0).reshape(1, 1, BS)
    weighted = (items.astype(jnp.float32) * item_w[:, :, None]).astype(jnp.bfloat16)
    products = lax.dot_general(
        items, weighted, (((1,), (1,)), ((0,), (0,))), preferred_element_type=jnp.float32
    )
    diag = lax.psum_scatter(
        jnp.einsum("il,ikb->lkb", onehot, products, precision=lax.Precision.HIGHEST),
        "batch",
        scatter_dimension=0,
        tiled=True,
    )
    return (diag.reshape(1, 1, BS, BS), gradient)


def solution(mesh):
    in_specs = (
        P(("batch", "coef"), None, None, None, None),
        P("coef", "batch", None),
        P("batch", None),
        P("batch"),
        P(),
    )
    out_specs = (P("coef", "batch", None, None), P("coef", "batch", None))
    return jax.shard_map(shards, mesh=mesh, in_specs=in_specs, out_specs=out_specs, check_vma=False)
```

profile of v0, /device:TPU:6, one launch (start us, length us, event | category | flops | bytes accessed | tf_op | source)
XLA Modules:
  0.0 338.0 jit_solution(15510032029880882865)
XLA Ops:
  7.2 0.0 copy-start.2
  7.2 0.0 copy-start.1
  7.2 0.0 copy-start.3
  7.2 3.2 copy.11
  10.4 9.4 %all-to-all-start = ((bf16[4,8,2,128,128]{4,3,2,0,1:T(8,128)(2,1)}), bf16[4,8,2,128,128]{4,3,2,0,1:T(8,128)(2,1)S(1)}, u32[]{:S(2)}, u32[]{:S(2)}) async-start(bf16[4,8,2,128,128]{4,3,2,0,1:T(8,128)(2,1)} %copy.11), calls=%async_computation | async-start | bytes 4194304 | tf_op jit(solution)/shard_map/all_to_all | solution.py:13
  19.8 0.0 reduce-scatter.2.cloned.1.call-start
  19.8 0.0 copy-done.2
  19.8 0.1 copy.10
  19.8 0.1 eq.15
  20.0 0.0 copy-done.1
  20.0 0.0 copy-done.3
  20.0 0.8 gather_fusion
  20.8 0.1 reshape.27
  20.9 0.1 broadcast_in_dim.14
  21.0 0.1 reshape.28
  21.1 20.6 %all-to-all-done = bf16[4,8,2,128,128]{4,3,2,0,1:T(8,128)(2,1)S(1)} async-done(((bf16[4,8,2,128,128]{4,3,2,0,1:T(8,128)(2,1)}), bf16[4,8,2,128,128]{4,3,2,0,1:T(8,128)(2,1)S(1)}, u32[]{:S(2)}, u32[]{:S(2)}) %all-to-all-start) | async-done | bytes 2097184 | tf_op jit(solution)/shard_map/all_to_all | solution.py:13
  41.7 4.2 %fusion.1 = f32[64,128,128]{1,2,0:T(8,128)} fusion(bf16[64,128,128]{2,1,0:T(8,128)(2,1)S(1)} %bitcast.25, f32[64,128]{1,0:T(8,128)S(1)} %bitcast.27), kind=kOutput, calls=%fused_computation.3 | convolution fusion | flops 271581184 | bytes 6324224 | tf_op jit(solution)/shard_map/dot_general | solution.py:28
  45.8 5.4 %copy.13 = f32[64,128,128]{2,0,1:T(8,128)} copy(f32[64,128,128]{1,2,0:T(8,128)} %fusion.1) | data formatting | bytes 8388608 | tf_op jit(solution)/shard_map/dot_general | solution.py:28
  51.2 4.6 %fusion.5 = f32[64,128,128]{2,0,1:T(8,128)S(1)} fusion(f32[64,128,128]{2,0,1:T(8,128)} %copy.13, s32[64]{0:T(128)S(1)} %eq.15), kind=kOutput, calls=%fused_computation.8 | convolution fusion | flops 805310464 | bytes 8388864 | tf_op jit(solution)/shard_map/il,ikb->lkb/dot_general | solution.py:32
  55.8 4.4 %copy.14 = f32[64,128,128]{2,1,0:T(8,128)} copy(f32[64,128,128]{2,0,1:T(8,128)S(1)} %fusion.5) | data formatting | bytes 8388608 | tf_op jit(solution)/shard_map/il,ikb->lkb/dot_general | solution.py:32
  60.2 0.0 copy-start
  60.2 0.0 reduce-scatter.2.cloned.1.call-update
  60.2 0.7 copy-done
  60.9 1.7 fusion.9
  62.7 0.1 fusion.3
  62.8 267.8 %psum.7 = f32[64,128]{1,0:T(8,128)S(1)} all-reduce(f32[64,128]{1,0:T(8,128)S(1)} %fusion.3), channel_id=1, replica_groups=mesh['batch'=64,'coef'=8] {'batch'}, use_global_device_ids=true, to_apply=%region_1.0 | all-reduce | flops 8192 | bytes 65536 | tf_op jit(solution)/shard_map/psum | solution.py:25
  330.7 0.5 dynamic-slice_bitcast_fusion
  331.2 0.0 reduce-scatter.2.cloned.1.call-done
  (6 shorter events, 0.0 us)
Async XLA Ops:
  7.2 12.6 %copy-start.2 = (s32[1,32,2]{1,2,0:T(2,128)S(1)}, s32[1,32,2]{1,2,0:T(2,128)}, u32[]{:S(2)}) copy-start(s32[1,32,2]{1,2,0:T(2,128)} %param.6) | copy-start | bytes 772
  7.2 12.8 %copy-start.1 = (bf16[4096]{0:T(1024)(128)(2,1)S(1)}, bf16[4096]{0:T(1024)(128)(2,1)}, u32[]{:S(2)}) copy-start(bf16[4096]{0:T(1024)(128)(2,1)} %param.9) | copy-start | bytes 24580
  7.2 12.8 %copy-start.3 = (s32[64]{0:T(128)S(1)}, s32[64]{0:T(128)}, u32[]{:S(2)}) copy-start(s32[64]{0:T(128)} %param.8) | copy-start | bytes 772
  10.4 31.3 %all-to-all-start = ((bf16[4,8,2,128,128]{4,3,2,0,1:T(8,128)(2,1)}), bf16[4,8,2,128,128]{4,3,2,0,1:T(8,128)(2,1)S(1)}, u32[]{:S(2)}, u32[]{:S(2)}) async-start(bf16[4,8,2,128,128]{4,3,2,0,1:T(8,128)(2,1)} %copy.11), calls=%async_computation | async-start | bytes 4194304 | tf_op jit(solution)/shard_map/all_to_all | solution.py:13
  19.8 311.4 %reduce-scatter.2.cloned.1.call-start = ((), (), s32[]{:S(2)}) async-start(), calls=%async_computation.2 | async-start | bytes 4259840 | tf_op jit(solution)/shard_map/reduce_scatter | solution.py:31
  60.2 0.7 copy-start
Sparse Core Ops, SparseCore 0:
  60.3 228.2 reduce-scatter.1
where the time goes:
time: 338 us
  blocking collectives  268 us (79%)
  waiting for transfers between devices  20.6 us (6%)
  local copies, waits for them, and re-layouts  15.5 us (5%)
  between operations  14.1 us (4%)
  matrix products  10.6 us (3%)
  starting transfers between devices  9.37 us (3%)
    psum x1, blocking collectives, shards(): gtotal = lax.psum(gpart, 'batch')  268 us
    all_to_all x1, waiting for transfers between devices, shards(): lax.all_to_all(jac_blocks, 'coef', split_axis=1, concat_axis=0, tiled=True)  20.6 us
    all_to_all x1, starting transfers between devices, shards(): lax.all_to_all(jac_blocks, 'coef', split_axis=1, concat_axis=0, tiled=True)  9.37 us
  transfers between devices with their start and end apart: 2, of which 1 were waited for; matrix products, arithmetic and copies ran while one was open for 1% of the time, Pallas kernels for 0%

commit v1 on v0

v1 whole, which is shorter than its diff:
```python
import functools

import jax
import jax.numpy as jnp
from jax import lax
from jax.experimental import pallas as pl
from jax.experimental.pallas import tpu as pltpu
from jax.sharding import Mesh
from jax.sharding import PartitionSpec as P

BS = 128
HALF = BS // 2
PAIR = 2
ROWS = HALF + 8
CODED = HALF + 16
FULL = 32000.0
STEPS = 16.0
TINY = 1e-30
VMEM = 48 * 1024 * 1024


def iota(shape, dim):
    return lax.broadcasted_iota(jnp.int32, shape, dim)


def products_kernel(unroll, targets, core, items, weights, residual, own, other, acc):
    n_items = items.shape[0]
    acc[...] = jnp.zeros_like(acc)
    upper = iota((HALF, BS), 1) >= iota((HALF, BS), 0)
    lanes = iota((HALF, BS), 1) == iota((HALF, BS), 0)
    sub = iota((8, BS), 0)

    def step(block, carry):
        for j in range(unroll):
            row = block * unroll + j
            w = weights[pl.ds(row, 1), :]
            wr = w * residual[pl.ds(row, 1), :]
            hi = wr.astype(jnp.bfloat16).astype(jnp.float32)
            mid = (wr - hi).astype(jnp.bfloat16).astype(jnp.float32)
            low = wr - hi - mid
            terms = jnp.where(sub == 0, hi, jnp.where(sub == 1, mid, jnp.where(sub == 2, low, 0.0)))
            terms = jnp.concatenate([terms, jnp.zeros_like(terms)], axis=0).astype(jnp.bfloat16)
            for s in range(PAIR):
                item = row * PAIR + s
                jac = items[item]
                scaled = (jac.T.astype(jnp.float32) * w).astype(jnp.bfloat16)
                left = jnp.concatenate([scaled, terms], axis=0)
                out = lax.dot_general(left, jac, (((1,), (0,)), ((), ())), preferred_element_type=jnp.float32)
                last = pltpu.roll(out[HALF:BS], HALF, 1)
                packed = jnp.where(upper, out[:HALF], last)
                diag = jnp.sum(jnp.where(lanes, last, 0.0), axis=0, keepdims=True)
                grad = jnp.sum(out[BS : BS + 8], axis=0, keepdims=True)
                tail = jnp.where(sub == 0, diag, jnp.where(sub == 1, grad, 0.0))
                where = targets[item]
                acc[where, :HALF] += packed
                acc[where, HALF:] += tail
        return carry

    lax.fori_loop(0, n_items // (PAIR * unroll), step, 0)
    me = core[0]

    def split(i, carry):
        own[i] = acc[2 * i + me]
        other[i] = acc[2 * i + 1 - me]
        return carry

    lax.fori_loop(0, own.shape[0], split, 0, unroll=4)


def encode_slot(value, coded, i):
    sub = iota((16, BS), 0)
    packed, tail = value[:HALF], value[HALF:]
    diag, grad = tail[0:1], tail[1:2]
    big = jnp.maximum(jnp.max(jnp.abs(packed), axis=0, keepdims=True), jnp.maximum(jnp.abs(diag), TINY))
    big_g = jnp.maximum(jnp.abs(grad), TINY)
    per = STEPS / 0.6931471805599453
    code = jnp.ceil(jnp.log(big) * per)
    code_g = jnp.ceil(jnp.log(big_g) * per)
    inv = jnp.exp2(code * (-1.0 / STEPS)) * FULL
    inv_g = jnp.exp2(code_g * (-1.0 / STEPS)) * FULL
    coded[i, :HALF] = jnp.round(packed * inv).astype(jnp.int32).astype(jnp.int16)
    g = grad * inv_g
    g_hi = jnp.round(g)
    g_lo = jnp.round((g - g_hi) * FULL)
    rows = [jnp.round(diag * inv), code, code_g, g_hi, g_lo]
    out = jnp.zeros((16, BS), jnp.float32)
    for k, row in enumerate(rows):
        out = jnp.where(sub == k, row, out)
    coded[i, HALF:] = out.astype(jnp.int32).astype(jnp.int16)


def add_kernel(unroll, own, got, coded):
    def step(block, carry):
        for j in range(unroll):
            i = block * unroll + j
            encode_slot(own[i] + got[i], coded, i)
        return carry

    lax.fori_loop(0, coded.shape[0] // unroll, step, 0)


def finish_kernel(coded, diag_out, grad_out):
    packed = jnp.zeros((HALF, BS), jnp.float32)
    diag = jnp.zeros((1, BS), jnp.float32)
    grad = jnp.zeros((1, BS), jnp.float32)
    for i in range(coded.shape[0]):
        tail = coded[i, HALF:].astype(jnp.int32).astype(jnp.float32)
        scale = jnp.exp2(tail[1:2] * (1.0 / STEPS)) * (1.0 / FULL)
        scale_g = jnp.exp2(tail[2:3] * (1.0 / STEPS)) * (1.0 / FULL)
        packed = packed + coded[i, :HALF].astype(jnp.int32).astype(jnp.float32) * scale
        diag = diag + tail[0:1] * scale
        grad = grad + (tail[3:4] + tail[4:5] * (1.0 / FULL)) * scale_g
    whole = jnp.concatenate([packed, pltpu.roll(packed, HALF, 1)], axis=0)
    flipped = whole.T
    r, c = iota((BS, BS), 0), iota((BS, BS), 1)
    plain = ((r < HALF) & (c >= r)) | ((c >= HALF) & (c < r))
    on = (r == c) & (r >= HALF)
    diag_out[...] = jnp.where(on, pltpu.roll(diag, HALF, 1), jnp.where(plain, whole, flipped))
    grad_out[...] = grad


def call(body, outs, scratch=(), smem=0, n_in=1, flops=0, moved=0):
    spec = pl.BlockSpec(memory_space=pltpu.VMEM)
    many = isinstance(outs, (list, tuple))
    return pl.pallas_call(
        body,
        out_shape=outs,
        in_specs=[pl.BlockSpec(memory_space=pltpu.SMEM)] * smem + [spec] * n_in,
        out_specs=[spec] * len(outs) if many else spec,
        scratch_shapes=list(scratch),
        compiler_params=pltpu.CompilerParams(vmem_limit_bytes=VMEM),
        cost_estimate=pl.CostEstimate(flops=flops, bytes_accessed=moved, transcendentals=0),
    )


def shards(jac_blocks, col_blocks, residual, run_of_half, run_scale):
    slots = lax.axis_size("z") * 4
    f32 = jnp.float32
    moved = lax.all_to_all(jac_blocks, "coef", split_axis=1, concat_axis=0, tiled=True)
    items = moved.reshape(-1, BS, BS)
    n_items = items.shape[0]
    targets = col_blocks.reshape(-1)
    scale_rows = run_scale.astype(f32)[run_of_half].reshape(-1, 2)
    weights = jnp.repeat(scale_rows, HALF, axis=1)
    me = lax.axis_index("core").astype(jnp.int32).reshape(1)
    piece = jax.ShapeDtypeStruct((slots // 2, ROWS, BS), f32)
    own, other = call(
        functools.partial(products_kernel, 2),
        [piece, piece],
        scratch=[pltpu.VMEM((slots, ROWS, BS), f32)],
        smem=2,
        n_in=3,
        flops=2 * n_items * BS**3,
        moved=n_items * BS * BS * 2 + slots * ROWS * BS * 4,
    )(targets, me, items, weights, residual)
    got = lax.ppermute(other, "core", [(0, 1), (1, 0)])
    coded = call(
        functools.partial(add_kernel, 4),
        jax.ShapeDtypeStruct((slots // 2, CODED, BS), jnp.int16),
        n_in=2,
        flops=slots * ROWS * BS * 8,
        moved=slots * ROWS * BS * 6,
    )(own, got)
    landed = lax.all_to_all(coded, ("z", "yh"), 0, 0, tiled=True)
    diag, grad = call(
        finish_kernel,
        [jax.ShapeDtypeStruct((BS, BS), f32), jax.ShapeDtypeStruct((1, BS), f32)],
        flops=slots * ROWS * BS * 4,
        moved=slots * ROWS * BS,
    )(landed)
    return diag.reshape(1, 1, BS, BS), grad.reshape(1, 1, BS)


def solution(mesh):
    fine = Mesh(mesh.devices.reshape(-1, 2, 2, mesh.devices.shape[1]), ("z", "yh", "core", "coef"))
    batch = ("z", "yh", "core")
    in_specs = (
        P(batch + ("coef",), None, None, None, None),
        P("coef", batch, None),
        P(batch, None),
        P(batch),
        P(),
    )
    out_specs = (P("coef", batch, None, None), P("coef", batch, None))
    return jax.shard_map(shards, mesh=fine, in_specs=in_specs, out_specs=out_specs, check_vma=False)
```

time: 338 us -> 106 us (0.31)
  blocking collectives: 268 us -> 58.3 us
  between operations: 14.1 us -> 0.72 us
  local copies, waits for them, and re-layouts: 15.5 us -> 4.44 us
  matrix products: 10.6 us -> 0 us
  Pallas kernels: 0 us -> 7.91 us
    psum x1 -> x0, blocking collectives: 268 us -> none  [shards(): gtotal = lax.psum(gpart, 'batch')]
    all_to_all x0 -> x1, blocking collectives: none -> 58.3 us  [shards(): landed = lax.all_to_all(coded, ('z', 'yh'), 0, 0, tiled=True)]
    dot_general x4 -> x0, matrix products: 10.6 us -> none  [the longest x1 4.58 us: shards(): jnp.einsum('il,ikb->lkb', onehot, products, precision=lax.Precision.HIGHEST)]
    dot_general x2 -> x0, local copies, waits for them, and re-layouts: 9.78 us -> none  [the longest x1 5.41 us: shards(): lax.dot_general(items, weighted, (((1,), (1,)), ((0,), (0,))), preferred_...]
    pallas_call x0 -> x3, Pallas kernels: none -> 7.91 us  [the longest x1 6.44 us: shards(): call(functools.partial(products_kernel, 2), [piece, piece], scratch=[pltp...]
  transfers between devices with their start and end apart: 2 -> 2, of which waited for: 1 -> 2; matrix products, arithmetic and copies ran while one was open for 1% -> 1% of each run, Pallas kernels for 0% -> 0%
where the time goes in v1:
time: 106 us
  blocking collectives  58.3 us (55%)
  waiting for transfers between devices  23.4 us (22%)
  starting transfers between devices  11.4 us (11%)
  Pallas kernels  7.91 us (7%)
  local copies, waits for them, and re-layouts  4.44 us (4%)
    all_to_all x1, blocking collectives, shards(): landed = lax.all_to_all(coded, ('z', 'yh'), 0, 0, tiled=True)  58.3 us
    all_to_all x1, waiting for transfers between devices, shards(): lax.all_to_all(jac_blocks, 'coef', split_axis=1, concat_axis=0, tiled=True)  20.6 us
    all_to_all x1, starting transfers between devices, shards(): lax.all_to_all(jac_blocks, 'coef', split_axis=1, concat_axis=0, tiled=True)  9.51 us
    pallas_call x1, Pallas kernels, shards(): call(functools.partial(products_kernel, 2), [piece, piece], scratch=[pltp...  6.44 us
    unnamed x10, local copies, waits for them, and re-layouts  3.29 us
    ppermute x1, waiting for transfers between devices, shards(): got = lax.ppermute(other, 'core', [(0, 1), (1, 0)])  2.81 us
  transfers between devices with their start and end apart: 2, of which 2 were waited for; matrix products, arithmetic and copies ran while one was open for 1% of the time, Pallas kernels for 0%

profile of v1, /device:TPU:6, one launch (start us, length us, event | category | flops | bytes accessed | tf_op | source)
XLA Modules:
  0.0 106.2 jit_solution(5250694049958057867)
XLA Ops:
  0.6 3.2 %copy.12 = bf16[4,8,2,128,128]{4,3,2,0,1:T(8,128)(2,1)} copy(bf16[4,8,2,128,128]{4,3,2,1,0:T(8,128)(2,1)} %param.5) | data formatting | bytes 4194304 | tf_op args[0]
  3.8 0.0 copy-start.2
  3.8 0.0 copy-start.1
  3.8 0.0 copy-start.3
  3.8 0.0 copy-start
  3.8 9.5 %all-to-all-start = ((bf16[4,8,2,128,128]{4,3,2,0,1:T(8,128)(2,1)}), bf16[4,8,2,128,128]{4,3,2,0,1:T(8,128)(2,1)S(1)}, u32[]{:S(2)}, u32[]{:S(2)}) async-start(bf16[4,8,2,128,128]{4,3,2,0,1:T(8,128)(2,1)} %copy.12), calls=%async_computation | async-start | bytes 4194304 | tf_op jit(solution)/shard_map/all_to_all | solution.py:139
  13.3 0.0 copy-done.2
  13.3 0.1 copy.11
  13.4 0.1 reshape.26.targets
  13.5 0.0 copy-done.1
  13.6 0.0 copy-done.3
  13.6 0.8 gather_fusion
  14.4 0.1 reshape.29
  14.5 0.1 broadcast_in_dim.7
  14.6 0.1 reshape.30.weights
  14.7 20.6 %all-to-all-done = bf16[4,8,2,128,128]{4,3,2,0,1:T(8,128)(2,1)S(1)} async-done(((bf16[4,8,2,128,128]{4,3,2,0,1:T(8,128)(2,1)}), bf16[4,8,2,128,128]{4,3,2,0,1:T(8,128)(2,1)S(1)}, u32[]{:S(2)}, u32[]{:S(2)}) %all-to-all-start) | async-done | bytes 2097184 | tf_op jit(solution)/shard_map/all_to_all | solution.py:139
  35.2 0.0 copy-done
  35.2 6.4 %shard_map.68 = (f32[32,72,128]{2,1,0:T(8,128)S(1)}, f32[32,72,128]{2,1,0:T(8,128)S(1)}) custom-call(s32[64]{0:T(128)S(1)} %reshape.26.targets, s32[1]{0:T(128)} %bitcast.core, bf16[64,128,128]{2,1,0:T(8,128)(2,1)S(1)} %bitcast.8, f32[32,128]{1,0:T(8,128)S(1)} %reshape.30.weights, f32[32,128]{1,0:T(8,128)S(1)} %copy-done), custom_call_target="tpu_custom_call" | custom-call | flops 268435456 | bytes 4456448 | tf_op jit(solution)/shard_map/pallas_call | solution.py:147
  41.7 1.9 %collective-permute-start = (f32[32,72,128]{2,1,0:T(8,128)S(1)}, f32[32,72,128]{2,1,0:T(8,128)S(1)}, u32[]{:S(2)}, u32[]{:S(2)}) collective-permute-start(f32[32,72,128]{2,1,0:T(8,128)S(1)} %get-tuple-element.7), channel_id=1, source_target_pairs={{0,8},{8,0},{1,9},{9,1},{2,10},{10,2},{3,11},{11,3},{4,12},{12,4},... | collective-permute-start | bytes 3538952 | tf_op jit(solution)/shard_map/ppermute | solution.py:156
  43.6 2.8 %collective-permute-done.got = f32[32,72,128]{2,1,0:T(8,128)S(1)} collective-permute-done((f32[32,72,128]{2,1,0:T(8,128)S(1)}, f32[32,72,128]{2,1,0:T(8,128)S(1)}, u32[]{:S(2)}, u32[]{:S(2)}) %collective-permute-start) | collective-permute-done | bytes 1179680 | tf_op jit(solution)/shard_map/ppermute | solution.py:156
  46.4 0.5 shard_map.69
  47.0 58.3 %all_to_all.20.coded = s16[32,80,128]{2,1,0:T(8,128)(2,1)S(1)} all-to-all(s16[32,80,128]{2,1,0:T(8,128)(2,1)S(1)} %shard_map.69), channel_id=1, replica_groups=mesh['z'=16,'yh'=2,'core'=2,'coef'=8] {'z','yh'}, dimensions={0} | all-to-all | bytes 1310720 | tf_op jit(solution)/shard_map/all_to_all | solution.py:164
  105.2 0.9 shard_map.70
  (3 shorter events, 0.0 us)
Async XLA Ops:
  3.8 9.5 %copy-start.2 = (s32[1,32,2]{1,2,0:T(2,128)S(1)}, s32[1,32,2]{1,2,0:T(2,128)}, u32[]{:S(2)}) copy-start(s32[1,32,2]{1,2,0:T(2,128)} %param.6) | copy-start | bytes 772
  3.8 9.7 %copy-start.1 = (bf16[4096]{0:T(1024)(128)(2,1)S(1)}, bf16[4096]{0:T(1024)(128)(2,1)}, u32[]{:S(2)}) copy-start(bf16[4096]{0:T(1024)(128)(2,1)} %param.9) | copy-start | bytes 24580
  3.8 9.7 %copy-start.3 = (s32[64]{0:T(128)S(1)}, s32[64]{0:T(128)}, u32[]{:S(2)}) copy-start(s32[64]{0:T(128)} %param.8) | copy-start | bytes 772
  3.8 31.4 %copy-start = (f32[32,128]{1,0:T(8,128)S(1)}, f32[32,128]{1,0:T(8,128)}, u32[]{:S(2)}) copy-start(f32[32,128]{1,0:T(8,128)} %residual.1) | copy-start | bytes 49156
  3.8 31.4 %all-to-all-start = ((bf16[4,8,2,128,128]{4,3,2,0,1:T(8,128)(2,1)}), bf16[4,8,2,128,128]{4,3,2,0,1:T(8,128)(2,1)S(1)}, u32[]{:S(2)}, u32[]{:S(2)}) async-start(bf16[4,8,2,128,128]{4,3,2,0,1:T(8,128)(2,1)} %copy.12), calls=%async_computation | async-start | bytes 4194304 | tf_op jit(solution)/shard_map/all_to_all | solution.py:139
  41.7 4.7 %collective-permute-start = (f32[32,72,128]{2,1,0:T(8,128)S(1)}, f32[32,72,128]{2,1,0:T(8,128)S(1)}, u32[]{:S(2)}, u32[]{:S(2)}) collective-permute-start(f32[32,72,128]{2,1,0:T(8,128)S(1)} %get-tuple-element.7), channel_id=1, source_target_pairs={{0,8},{8,0},{1,9},{9,1},{2,10},{10,2},{3,11},{11,3},{4,12},{12,4},... | collective-permute-start | bytes 3538952 | tf_op jit(solution)/shard_map/ppermute | solution.py:156

commit v2 on v1

v2 whole, which is shorter than its diff:
```python
import functools
import math

import jax
import jax.numpy as jnp
from jax import lax
from jax.experimental import pallas as pl
from jax.experimental.pallas import tpu as pltpu
from jax.sharding import Mesh
from jax.sharding import PartitionSpec as P

BS = 128
HALF = BS // 2
PAIR = 2
ROWS = HALF + 8
FULL = 32000.0
STEPS = 16.0
TINY = 1e-30
VMEM = 48 * 1024 * 1024
PER = STEPS / 0.6931471805599453


def iota(shape, dim):
    return lax.broadcasted_iota(jnp.int32, shape, dim)


def stack_rows(rows):
    sub = iota((8, BS), 0)
    out = jnp.zeros((8, BS), jnp.float32)
    for k, row in enumerate(rows):
        out = jnp.where(sub == k, row, out)
    return out


def to_int16(x):
    return jnp.round(x).astype(jnp.int32).astype(jnp.int16)


def loop(n, unroll, body):
    unroll = math.gcd(n, unroll)

    def step(block, carry):
        for j in range(unroll):
            body(block * unroll + j)
        return carry

    lax.fori_loop(0, n // unroll, step, 0)


def encode(packed, diag, grad):
    big = jnp.maximum(jnp.max(jnp.abs(packed), axis=0, keepdims=True), jnp.maximum(jnp.abs(diag), TINY))
    big_g = jnp.maximum(jnp.abs(grad), TINY)
    code = jnp.ceil(jnp.log(big) * PER)
    code_g = jnp.ceil(jnp.log(big_g) * PER)
    inv = jnp.exp2(code * (-1.0 / STEPS)) * FULL
    inv_g = jnp.exp2(code_g * (-1.0 / STEPS)) * FULL
    g = grad * inv_g
    g_hi = jnp.round(g)
    g_lo = (g - g_hi) * FULL
    return to_int16(packed * inv), to_int16(stack_rows([diag * inv, code, code_g, g_hi, g_lo]))


def decode(main, tail):
    tail = tail.astype(jnp.int32).astype(jnp.float32)
    scale = jnp.exp2(tail[1:2] * (1.0 / STEPS)) * (1.0 / FULL)
    scale_g = jnp.exp2(tail[2:3] * (1.0 / STEPS)) * (1.0 / FULL)
    packed = main.astype(jnp.int32).astype(jnp.float32) * scale
    return packed, tail[0:1] * scale, (tail[3:4] + tail[4:5] * (1.0 / FULL)) * scale_g


def products_kernel(unroll, place, weights, residual, jac_hbm, coded, jac, sem):
    n_rows, groups = jac_hbm.shape[:2]
    copies = [pltpu.make_async_copy(jac_hbm.at[r], jac.at[r], sem.at[r]) for r in range(n_rows)]
    for copy in copies:
        copy.start()
    upper = iota((HALF, BS), 1) >= iota((HALF, BS), 0)
    lanes = iota((HALF, BS), 1) == iota((HALF, BS), 0)
    for r in range(n_rows):
        w = weights[pl.ds(r, 1), :]
        wr = w * residual[pl.ds(place[0] * n_rows + r, 1), :]
        hi = wr.astype(jnp.bfloat16).astype(jnp.float32)
        mid = (wr - hi).astype(jnp.bfloat16).astype(jnp.float32)
        terms = stack_rows([hi, mid, wr - hi - mid])
        terms = jnp.concatenate([terms, jnp.zeros_like(terms)], axis=0).astype(jnp.bfloat16)
        copies[r].wait()

        def body(g):
            for s in range(PAIR):
                one = jac[r, g, s]
                scaled = (one.T.astype(jnp.float32) * w).astype(jnp.bfloat16)
                left = jnp.concatenate([scaled, terms], axis=0)
                out = lax.dot_general(left, one, (((1,), (0,)), ((), ())), preferred_element_type=jnp.float32)
                last = pltpu.roll(out[HALF:BS], HALF, 1)
                packed = jnp.where(upper, out[:HALF], last)
                diag = jnp.sum(jnp.where(lanes, last, 0.0), axis=0, keepdims=True)
                grad = jnp.sum(out[BS : BS + 8], axis=0, keepdims=True)
                main, tail = encode(packed, diag, grad)
                coded[g, r * PAIR + s, :HALF] = main
                coded[g, r * PAIR + s, HALF:] = tail

        loop(groups, unroll, body)


def place_kernel(unroll, targets, core, coded, own, other, acc):
    acc[...] = jnp.zeros_like(acc)

    def body(i):
        packed, diag, grad = decode(coded[i, :HALF], coded[i, HALF:])
        where = targets[i]
        acc[where, :HALF] += packed
        acc[where, HALF:] += stack_rows([diag, grad])

    loop(coded.shape[0], unroll, body)
    me = core[0]

    def split(i):
        own[i] = acc[2 * i + me]
        other[i] = acc[2 * i + 1 - me]

    loop(own.shape[0], unroll, split)


def halve_kernel(unroll, part, own, got, kept, coded):
    me = part[0]

    def body(i):
        mine, theirs = 2 * i + me, 2 * i + 1 - me
        kept[i] = own[mine] + got[mine]
        value = own[theirs] + got[theirs]
        coded[i, :HALF], coded[i, HALF:] = encode(value[:HALF], value[HALF : HALF + 1], value[HALF + 1 : HALF + 2])

    loop(coded.shape[0], unroll, body)


def recode_kernel(unroll, kept, got, coded):
    def body(i):
        packed, diag, grad = decode(got[i, :HALF], got[i, HALF:])
        tail = kept[i, HALF:]
        coded[i, :HALF], coded[i, HALF:] = encode(kept[i, :HALF] + packed, tail[0:1] + diag, tail[1:2] + grad)

    loop(coded.shape[0], unroll, body)


def finish_kernel(coded, diag_out, grad_out):
    packed = jnp.zeros((HALF, BS), jnp.float32)
    diag = jnp.zeros((1, BS), jnp.float32)
    grad = jnp.zeros((1, BS), jnp.float32)
    for i in range(coded.shape[0]):
        more = decode(coded[i, :HALF], coded[i, HALF:])
        packed, diag, grad = packed + more[0], diag + more[1], grad + more[2]
    whole = jnp.concatenate([packed, pltpu.roll(packed, HALF, 1)], axis=0)
    flipped = whole.T
    r, c = iota((BS, BS), 0), iota((BS, BS), 1)
    plain = ((r < HALF) & (c >= r)) | ((c >= HALF) & (c < r))
    on = (r == c) & (r >= HALF)
    diag_out[...] = jnp.where(on, pltpu.roll(diag, HALF, 1), jnp.where(plain, whole, flipped))
    grad_out[...] = grad


def call(body, outs, specs, scratch=(), flops=0, moved=0):
    spaces = {"v": pltpu.VMEM, "s": pltpu.SMEM, "a": pl.ANY}
    spec = pl.BlockSpec(memory_space=pltpu.VMEM)
    many = isinstance(outs, (list, tuple))
    return pl.pallas_call(
        body,
        out_shape=outs,
        in_specs=[pl.BlockSpec(memory_space=spaces[k]) for k in specs],
        out_specs=[spec] * len(outs) if many else spec,
        scratch_shapes=list(scratch),
        compiler_params=pltpu.CompilerParams(vmem_limit_bytes=VMEM),
        cost_estimate=pl.CostEstimate(flops=flops, bytes_accessed=moved, transcendentals=0),
    )


def shards(jac_blocks, col_blocks, residual, run_of_half, run_scale):
    f32, i16 = jnp.float32, jnp.int16
    slots = lax.axis_size("z") * 4
    n_rows, groups = jac_blocks.shape[:2]
    n_items = n_rows * groups * PAIR

    def index(name):
        return lax.axis_index(name).astype(jnp.int32).reshape(1)

    def shape(n, dtype):
        return jax.ShapeDtypeStruct((n, ROWS, BS), dtype)

    coef = index("coef")
    runs = lax.dynamic_slice_in_dim(run_of_half, coef[0] * n_rows * 2, n_rows * 2)
    weights = jnp.repeat(run_scale[runs].astype(f32).reshape(n_rows, 2), HALF, axis=1)
    coded = call(
        functools.partial(products_kernel, 2),
        jax.ShapeDtypeStruct((groups, n_rows * PAIR, ROWS, BS), i16),
        "svva",
        scratch=[pltpu.VMEM(jac_blocks.shape, jnp.bfloat16), pltpu.SemaphoreType.DMA((n_rows,))],
        flops=2 * n_items * BS**3,
        moved=n_items * BS * BS * 3,
    )(coef, weights, residual, jac_blocks)
    landed = lax.all_to_all(coded, "coef", 0, 0, tiled=True).reshape(n_items, ROWS, BS)
    own, other = call(
        functools.partial(place_kernel, 4),
        [shape(slots // 2, f32)] * 2,
        "ssv",
        scratch=[pltpu.VMEM((slots, ROWS, BS), f32)],
    )(col_blocks.reshape(-1), index("core"), landed)
    got = lax.ppermute(other, "core", [(0, 1), (1, 0)])
    kept, coded = call(
        functools.partial(halve_kernel, 4), [shape(slots // 4, f32), shape(slots // 4, i16)], "svv"
    )(index("yh"), own, got)
    got = lax.ppermute(coded, "yh", [(0, 1), (1, 0)])
    coded = call(functools.partial(recode_kernel, 4), shape(slots // 4, i16), "vv")(kept, got)
    landed = lax.all_to_all(coded, "z", 0, 0, tiled=True)
    diag, grad = call(
        finish_kernel, [jax.ShapeDtypeStruct((BS, BS), f32), jax.ShapeDtypeStruct((1, BS), f32)], "v"
    )(landed)
    return diag.reshape(1, 1, BS, BS), grad.reshape(1, 1, BS)


def solution(mesh):
    fine = Mesh(mesh.devices.reshape(-1, 2, 2, mesh.devices.shape[1]), ("z", "yh", "core", "coef"))
    batch = ("z", "yh", "core")
    in_specs = (
        P(batch + ("coef",), None, None, None, None),
        P("coef", batch, None),
        P(batch, None),
        P(batch),
        P(),
    )
    out_specs = (P("coef", batch, None, None), P("coef", batch, None))
    return jax.shard_map(shards, mesh=fine, in_specs=in_specs, out_specs=out_specs, check_vma=False)
```

time: 106 us -> 89 us (0.84)
  the two profiles are of different devices: /device:TPU:6 before, /device:TPU:16 now
where the time goes in v2:
time: 89 us; the launch traced here: 88.7 us
  blocking collectives  34.4 us (39%)
  waiting for transfers between devices  29.6 us (33%)
  Pallas kernels  10.2 us (11%)
  starting transfers between devices  9.49 us (11%)
  local copies, waits for them, and re-layouts  3.42 us (4%)
    all_to_all x1, blocking collectives, shards(): landed = lax.all_to_all(coded, 'z', 0, 0, tiled=True)  34.4 us
    all_to_all x1, waiting for transfers between devices, shards(): lax.all_to_all(coded, 'coef', 0, 0, tiled=True).reshape(n_items, ROWS, BS)  16.9 us
    ppermute x1, waiting for transfers between devices, shards(): got = lax.ppermute(coded, 'yh', [(0, 1), (1, 0)])  9.9 us
    pallas_call x1, Pallas kernels, shards(): call(functools.partial(products_kernel, 2), jax.ShapeDtypeStruct((groups,...  7.27 us
    all_to_all x1, starting transfers between devices, shards(): lax.all_to_all(coded, 'coef', 0, 0, tiled=True).reshape(n_items, ROWS, BS)  5.03 us
    ppermute x1, waiting for transfers between devices, shards(): got = lax.ppermute(other, 'core', [(0, 1), (1, 0)])  2.81 us
    ppermute x1, starting transfers between devices, shards(): got = lax.ppermute(coded, 'yh', [(0, 1), (1, 0)])  2.54 us
    unnamed x9, local copies, waits for them, and re-layouts  2.42 us
  transfers between devices with their start and end apart: 3, of which 3 were waited for; matrix products, arithmetic and copies ran while one was open for 0% of the time, Pallas kernels for 0%

profile of v2, /device:TPU:16, one launch (start us, length us, event | category | flops | bytes accessed | tf_op | source)
XLA Modules:
  0.0 88.7 jit_solution(6264573376985028706)
XLA Ops:
  0.6 0.0 copy-start
  0.7 0.7 compare_select_fusion
  1.4 0.0 copy-done
  1.4 0.6 gather_fusion
  2.0 0.1 reshape.40
  2.1 0.1 broadcast_in_dim.7
  2.2 0.1 reshape.36.weights
  2.3 0.0 copy-start.1
  2.3 1.6 %copy-done.1 = bf16[4,8,2,128,128]{4,3,2,1,0:T(8,128)(2,1)S(1)} copy-done((bf16[4,8,2,128,128]{4,3,2,1,0:T(8,128)(2,1)S(1)}, bf16[4,8,2,128,128]{4,3,2,1,0:T(8,128)(2,1)}, u32[]{:S(2)}) %copy-start.1) | copy-done | bytes 2097176
  3.9 0.0 copy-start.2
  3.9 0.7 copy-done.2
  4.6 7.3 %shard_map.68 = s16[8,8,72,128]{3,2,1,0:T(8,128)(2,1)} custom-call(s32[1]{0:T(128)} %bitcast.2.place, f32[4,128]{1,0:T(4,128)S(1)} %reshape.36.weights, f32[32,128]{1,0:T(8,128)S(1)} %copy-done.2, bf16[4,8,2,128,128]{4,3,2,1,0:T(8,128)(2,1)S(1)} %copy-done.1), custom_call_target="tpu_custom_call" | custom-call | flops 268435456 | bytes 3145728 | tf_op jit(solution)/shard_map/pallas_call | solution.py:190
  11.9 0.0 copy-start.3
  11.9 5.0 %all-to-all-start = ((s16[8,8,72,128]{3,2,1,0:T(8,128)(2,1)}), s16[8,8,72,128]{3,2,1,0:T(8,128)(2,1)S(1)}, u32[]{:S(2)}, u32[]{:S(2)}) async-start(s16[8,8,72,128]{3,2,1,0:T(8,128)(2,1)} %shard_map.68), calls=%async_computation | async-start | bytes 2359296 | tf_op jit(solution)/shard_map/all_to_all | solution.py:198
  16.9 0.0 copy-done.3
  16.9 0.1 copy.8
  17.0 0.1 reshape.33.targets
  17.1 16.9 %all-to-all-done = s16[8,8,72,128]{3,2,1,0:T(8,128)(2,1)S(1)} async-done(((s16[8,8,72,128]{3,2,1,0:T(8,128)(2,1)}), s16[8,8,72,128]{3,2,1,0:T(8,128)(2,1)S(1)}, u32[]{:S(2)}, u32[]{:S(2)}) %all-to-all-start) | async-done | bytes 1179680 | tf_op jit(solution)/shard_map/all_to_all | solution.py:198
  34.0 1.5 %shard_map.69 = (f32[32,72,128]{2,1,0:T(8,128)S(1)}, f32[32,72,128]{2,1,0:T(8,128)S(1)}) custom-call(s32[64]{0:T(128)S(1)} %reshape.33.targets, s32[1]{0:T(128)} %bitcast.1.core, s16[64,72,128]{2,1,0:T(8,128)(2,1)S(1)} %bitcast.6), custom_call_target="tpu_custom_call" | custom-call | tf_op jit(solution)/shard_map/pallas_call | solution.py:199
  35.5 1.9 %collective-permute-start = (f32[32,72,128]{2,1,0:T(8,128)S(1)}, f32[32,72,128]{2,1,0:T(8,128)S(1)}, u32[]{:S(2)}, u32[]{:S(2)}) collective-permute-start(f32[32,72,128]{2,1,0:T(8,128)S(1)} %get-tuple-element.9), channel_id=1, source_target_pairs={{0,8},{8,0},{1,9},{9,1},{2,10},{10,2},{3,11},{11,3},{4,12},{12,4},... | collective-permute-start | bytes 3538952 | tf_op jit(solution)/shard_map/ppermute | solution.py:205
  37.5 2.8 %collective-permute-done.got = f32[32,72,128]{2,1,0:T(8,128)S(1)} collective-permute-done((f32[32,72,128]{2,1,0:T(8,128)S(1)}, f32[32,72,128]{2,1,0:T(8,128)S(1)}, u32[]{:S(2)}, u32[]{:S(2)}) %collective-permute-start) | collective-permute-done | bytes 1179680 | tf_op jit(solution)/shard_map/ppermute | solution.py:205
  40.3 0.3 shard_map.70
  40.6 2.5 %collective-permute-start.1 = (s16[16,72,128]{2,1,0:T(8,128)(2,1)S(1)}, s16[16,72,128]{2,1,0:T(8,128)(2,1)S(1)}, u32[]{:S(2)}, u32[]{:S(2)}) collective-permute-start(s16[16,72,128]{2,1,0:T(8,128)(2,1)S(1)} %get-tuple-element.11), channel_id=1, source_target_pairs={{0,16},{16,0},{1,17},{17,1},{2,18},{18,2},{3,19},{19,3},{4,20},{20... | collective-permute-start | bytes 884744 | tf_op jit(solution)/shard_map/ppermute | solution.py:209
  43.1 9.9 %collective-permute-done.1.got = s16[16,72,128]{2,1,0:T(8,128)(2,1)S(1)} collective-permute-done((s16[16,72,128]{2,1,0:T(8,128)(2,1)S(1)}, s16[16,72,128]{2,1,0:T(8,128)(2,1)S(1)}, u32[]{:S(2)}, u32[]{:S(2)}) %collective-permute-start.1) | collective-permute-done | bytes 294944 | tf_op jit(solution)/shard_map/ppermute | solution.py:209
  53.0 0.3 shard_map.71
  53.4 34.4 %all_to_all.10.coded = s16[16,72,128]{2,1,0:T(8,128)(2,1)S(1)} all-to-all(s16[16,72,128]{2,1,0:T(8,128)(2,1)S(1)} %shard_map.71), channel_id=1, replica_groups=mesh['z'=16,'yh'=2,'core'=2,'coef'=8] {'z'}, dimensions={0} | all-to-all | bytes 589824 | tf_op jit(solution)/shard_map/all_to_all | solution.py:211
  87.8 0.9 shard_map.72
  (1 shorter events, 0.0 us)
Async XLA Ops:
  0.6 0.8 copy-start
  2.3 1.6 %copy-start.1 = (bf16[4,8,2,128,128]{4,3,2,1,0:T(8,128)(2,1)S(1)}, bf16[4,8,2,128,128]{4,3,2,1,0:T(8,128)(2,1)}, u32[]{:S(2)}) copy-start(bf16[4,8,2,128,128]{4,3,2,1,0:T(8,128)(2,1)} %jac_hbm.1) | copy-start | bytes 6291460
  3.9 0.7 copy-start.2
  11.9 5.0 %copy-start.3 = (s32[1,32,2]{1,2,0:T(2,128)S(1)}, s32[1,32,2]{1,2,0:T(2,128)}, u32[]{:S(2)}) copy-start(s32[1,32,2]{1,2,0:T(2,128)} %param.6) | copy-start | bytes 772
  11.9 22.1 %all-to-all-start = ((s16[8,8,72,128]{3,2,1,0:T(8,128)(2,1)}), s16[8,8,72,128]{3,2,1,0:T(8,128)(2,1)S(1)}, u32[]{:S(2)}, u32[]{:S(2)}) async-start(s16[8,8,72,128]{3,2,1,0:T(8,128)(2,1)} %shard_map.68), calls=%async_computation | async-start | bytes 2359296 | tf_op jit(solution)/shard_map/all_to_all | solution.py:198
  35.5 4.7 %collective-permute-start = (f32[32,72,128]{2,1,0:T(8,128)S(1)}, f32[32,72,128]{2,1,0:T(8,128)S(1)}, u32[]{:S(2)}, u32[]{:S(2)}) collective-permute-start(f32[32,72,128]{2,1,0:T(8,128)S(1)} %get-tuple-element.9), channel_id=1, source_target_pairs={{0,8},{8,0},{1,9},{9,1},{2,10},{10,2},{3,11},{11,3},{4,12},{12,4},... | collective-permute-start | bytes 3538952 | tf_op jit(solution)/shard_map/ppermute | solution.py:205
  40.6 12.4 %collective-permute-start.1 = (s16[16,72,128]{2,1,0:T(8,128)(2,1)S(1)}, s16[16,72,128]{2,1,0:T(8,128)(2,1)S(1)}, u32[]{:S(2)}, u32[]{:S(2)}) collective-permute-start(s16[16,72,128]{2,1,0:T(8,128)(2,1)S(1)} %get-tuple-element.11), channel_id=1, source_target_pairs={{0,16},{16,0},{1,17},{17,1},{2,18},{18,2},{3,19},{19,3},{4,20},{20... | collective-permute-start | bytes 884744 | tf_op jit(solution)/shard_map/ppermute | solution.py:209

commit v3 on v2

--- a/solution.py
+++ b/solution.py
@@ -16,7 +16,6 @@
 FULL = 32000.0
 STEPS = 16.0
 TINY = 1e-30
-VMEM = 48 * 1024 * 1024
 PER = STEPS / 0.6931471805599453
 
 
@@ -68,16 +67,32 @@
     return packed, tail[0:1] * scale, (tail[3:4] + tail[4:5] * (1.0 / FULL)) * scale_g
 
 
-def products_kernel(unroll, place, weights, residual, jac_hbm, coded, jac, sem):
+def products_kernel(unroll, place, runs, scales_hbm, residual_hbm, jac_hbm, out_hbm, jac, coded, scales, residual, table, sem, out_sem, aux_sem):
     n_rows, groups = jac_hbm.shape[:2]
     copies = [pltpu.make_async_copy(jac_hbm.at[r], jac.at[r], sem.at[r]) for r in range(n_rows)]
-    for copy in copies:
+    aux = [
+        pltpu.make_async_copy(scales_hbm, scales, aux_sem.at[0]),
+        pltpu.make_async_copy(residual_hbm, residual, aux_sem.at[1]),
+    ]
+    for copy in aux + copies:
         copy.start()
+    done = []
+    for copy in aux:
+        copy.wait()
+    table[...] = scales[...].astype(jnp.float32)
     upper = iota((HALF, BS), 1) >= iota((HALF, BS), 0)
     lanes = iota((HALF, BS), 1) == iota((HALF, BS), 0)
+    lane = iota((1, BS), 1)
+
+    def scale(half):
+        run = runs[half]
+        line = table[pl.ds(lax.div(run, BS), 1), :]
+        return jnp.sum(jnp.where(lane == lax.rem(run, BS), line, 0.0), axis=1, keepdims=True)
+
     for r in range(n_rows):
-        w = weights[pl.ds(r, 1), :]
-        wr = w * residual[pl.ds(place[0] * n_rows + r, 1), :]
+        row = place[0] * n_rows + r
+        w = jnp.where(lane < HALF, scale(2 * row), scale(2 * row + 1))
+        wr = w * residual[pl.ds(row, 1), :]
         hi = wr.astype(jnp.bfloat16).astype(jnp.float32)
         mid = (wr - hi).astype(jnp.bfloat16).astype(jnp.float32)
         terms = stack_rows([hi, mid, wr - hi - mid])
@@ -95,10 +110,14 @@
                 diag = jnp.sum(jnp.where(lanes, last, 0.0), axis=0, keepdims=True)
                 grad = jnp.sum(out[BS : BS + 8], axis=0, keepdims=True)
                 main, tail = encode(packed, diag, grad)
-                coded[g, r * PAIR + s, :HALF] = main
-                coded[g, r * PAIR + s, HALF:] = tail
+                coded[r, g, s, :HALF] = main
+                coded[r, g, s, HALF:] = tail
 
         loop(groups, unroll, body)
+        done.append(pltpu.make_async_copy(coded.at[r], out_hbm.at[:, r], out_sem.at[r]))
+        done[-1].start()
+    for copy in done:
+        copy.wait()
 
 
 def place_kernel(unroll, targets, core, coded, own, other, acc):
@@ -115,7 +134,8 @@
 
     def split(i):
         own[i] = acc[2 * i + me]
-        other[i] = acc[2 * i + 1 - me]
+        value = acc[2 * i + 1 - me]
+        other[i, :HALF], other[i, HALF:] = encode(value[:HALF], value[HALF : HALF + 1], value[HALF + 1 : HALF + 2])
 
     loop(own.shape[0], unroll, split)
 
@@ -125,9 +145,12 @@
 
     def body(i):
         mine, theirs = 2 * i + me, 2 * i + 1 - me
-        kept[i] = own[mine] + got[mine]
-        value = own[theirs] + got[theirs]
-        coded[i, :HALF], coded[i, HALF:] = encode(value[:HALF], value[HALF : HALF + 1], value[HALF + 1 : HALF + 2])
+        packed, diag, grad = decode(got[mine, :HALF], got[mine, HALF:])
+        kept[i, :HALF] = own[mine, :HALF] + packed
+        kept[i, HALF:] = own[mine, HALF:] + stack_rows([diag, grad])
+        packed, diag, grad = decode(got[theirs, :HALF], got[theirs, HALF:])
+        tail = own[theirs, HALF:]
+        coded[i, :HALF], coded[i, HALF:] = encode(own[theirs, :HALF] + packed, tail[0:1] + diag, tail[1:2] + grad)
 
     loop(coded.shape[0], unroll, body)
 
@@ -157,9 +180,9 @@
     grad_out[...] = grad
 
 
-def call(body, outs, specs, scratch=(), flops=0, moved=0):
-    spaces = {"v": pltpu.VMEM, "s": pltpu.SMEM, "a": pl.ANY}
-    spec = pl.BlockSpec(memory_space=pltpu.VMEM)
+def call(body, outs, specs, out="v", vmem=32, scratch=(), flops=0, moved=0):
+    spaces = {"v": pltpu.VMEM, "s": pltpu.SMEM, "h": pltpu.HBM}
+    spec = pl.BlockSpec(memory_space=spaces[out])
     many = isinstance(outs, (list, tuple))
     return pl.pallas_call(
         body,
@@ -167,7 +190,7 @@
         in_specs=[pl.BlockSpec(memory_space=spaces[k]) for k in specs],
         out_specs=[spec] * len(outs) if many else spec,
         scratch_shapes=list(scratch),
-        compiler_params=pltpu.CompilerParams(vmem_limit_bytes=VMEM),
+        compiler_params=pltpu.CompilerParams(vmem_limit_bytes=vmem * 1024 * 1024),
         cost_estimate=pl.CostEstimate(flops=flops, bytes_accessed=moved, transcendentals=0),
     )
 
@@ -184,30 +207,38 @@
     def shape(n, dtype):
         return jax.ShapeDtypeStruct((n, ROWS, BS), dtype)
 
-    coef = index("coef")
-    runs = lax.dynamic_slice_in_dim(run_of_half, coef[0] * n_rows * 2, n_rows * 2)
-    weights = jnp.repeat(run_scale[runs].astype(f32).reshape(n_rows, 2), HALF, axis=1)
     coded = call(
-        functools.partial(products_kernel, 2),
-        jax.ShapeDtypeStruct((groups, n_rows * PAIR, ROWS, BS), i16),
-        "svva",
-        scratch=[pltpu.VMEM(jac_blocks.shape, jnp.bfloat16), pltpu.SemaphoreType.DMA((n_rows,))],
+        functools.partial(products_kernel, 8),
+        jax.ShapeDtypeStruct((groups, n_rows, PAIR, ROWS, BS), i16),
+        "sshhh",
+        out="h",
+        vmem=60,
+        scratch=[
+            pltpu.VMEM(jac_blocks.shape, jnp.bfloat16),
+            pltpu.VMEM((n_rows, groups, PAIR, ROWS, BS), i16),
+            pltpu.VMEM((run_scale.shape[0] // BS, BS), jnp.bfloat16),
+            pltpu.VMEM(residual.shape, f32),
+            pltpu.VMEM((run_scale.shape[0] // BS, BS), f32),
+            pltpu.SemaphoreType.DMA((n_rows,)),
+            pltpu.SemaphoreType.DMA((n_rows,)),
+            pltpu.SemaphoreType.DMA((2,)),
+        ],
         flops=2 * n_items * BS**3,
         moved=n_items * BS * BS * 3,
-    )(coef, weights, residual, jac_blocks)
+    )(index("coef"), run_of_half, run_scale.reshape(-1, BS), residual, jac_blocks)
     landed = lax.all_to_all(coded, "coef", 0, 0, tiled=True).reshape(n_items, ROWS, BS)
     own, other = call(
-        functools.partial(place_kernel, 4),
-        [shape(slots // 2, f32)] * 2,
+        functools.partial(place_kernel, 8),
+        [shape(slots // 2, f32), shape(slots // 2, i16)],
         "ssv",
         scratch=[pltpu.VMEM((slots, ROWS, BS), f32)],
     )(col_blocks.reshape(-1), index("core"), landed)
     got = lax.ppermute(other, "core", [(0, 1), (1, 0)])
     kept, coded = call(
-        functools.partial(halve_kernel, 4), [shape(slots // 4, f32), shape(slots // 4, i16)], "svv"
+        functools.partial(halve_kernel, 8), [shape(slots // 4, f32), shape(slots // 4, i16)], "svv"
     )(index("yh"), own, got)
     got = lax.ppermute(coded, "yh", [(0, 1), (1, 0)])
-    coded = call(functools.partial(recode_kernel, 4), shape(slots // 4, i16), "vv")(kept, got)
+    coded = call(functools.partial(recode_kernel, 8), shape(slots // 4, i16), "vv")(kept, got)
     landed = lax.all_to_all(coded, "z", 0, 0, tiled=True)
     diag, grad = call(
         finish_kernel, [jax.ShapeDtypeStruct((BS, BS), f32), jax.ShapeDtypeStruct((1, BS), f32)], "v"

time: 89 us -> 82.6 us (0.928)
  local copies, waits for them, and re-layouts: 3.42 us -> 0.2 us
  Pallas kernels: 10.2 us -> 8.67 us
    unnamed x9 -> x3, local copies, waits for them, and re-layouts: 2.42 us -> 0.09 us
    pallas_call x4, Pallas kernels: 9.39 us -> 7.81 us  [the longest x1 5.4 us: shards(): call(functools.partial(products_kernel, 8), jax.ShapeDtypeStruct((groups,...]
where the time goes in v3:
time: 82.6 us; the launch traced here: 82.3 us
  blocking collectives  34.5 us (42%)
  waiting for transfers between devices  28.8 us (35%)
  starting transfers between devices  9.49 us (11%)
  Pallas kernels  8.67 us (10%)
    all_to_all x1, blocking collectives, shards(): landed = lax.all_to_all(coded, 'z', 0, 0, tiled=True)  34.5 us
    all_to_all x1, waiting for transfers between devices, shards(): lax.all_to_all(coded, 'coef', 0, 0, tiled=True).reshape(n_items, ROWS, BS)  16.9 us
    ppermute x1, waiting for transfers between devices, shards(): got = lax.ppermute(coded, 'yh', [(0, 1), (1, 0)])  9.91 us
    pallas_call x1, Pallas kernels, shards(): call(functools.partial(products_kernel, 8), jax.ShapeDtypeStruct((groups,...  5.4 us
    all_to_all x1, starting transfers between devices, shards(): lax.all_to_all(coded, 'coef', 0, 0, tiled=True).reshape(n_items, ROWS, BS)  5.04 us
    ppermute x1, starting transfers between devices, shards(): got = lax.ppermute(coded, 'yh', [(0, 1), (1, 0)])  2.53 us
    ppermute x1, waiting for transfers between devices, shards(): got = lax.ppermute(other, 'core', [(0, 1), (1, 0)])  1.97 us
    ppermute x1, starting transfers between devices, shards(): got = lax.ppermute(other, 'core', [(0, 1), (1, 0)])  1.92 us
  transfers between devices with their start and end apart: 3, of which 3 were waited for; matrix products, arithmetic and copies ran while one was open for 0% of the time, Pallas kernels for 0%

profile of v3, /device:TPU:16, one launch (start us, length us, event | category | flops | bytes accessed | tf_op | source)
XLA Modules:
  0.0 82.3 jit_solution(15034226416255568695)
XLA Ops:
  0.6 5.4 %shard_map.68 = s16[8,4,2,72,128]{4,3,2,1,0:T(8,128)(2,1)} custom-call(s32[1]{0:T(128)} %bitcast.2.place, s32[64]{0:T(128)} %runs.1, bf16[32,128]{1,0:T(8,128)(2,1)} %bitcast.8, f32[32,128]{1,0:T(8,128)} %residual_hbm.1, bf16[4,8,2,128,128]{4,3,2,1,0:T(8,128)(2,1)} %jac_hbm.1), custom_call_target="tpu_custom_call" | custom-call | flops 268435456 | bytes 3145728 | tf_op jit(solution)/shard_map/pallas_call | solution.py:210
  6.0 0.0 copy-start
  6.1 5.0 %all-to-all-start = ((s16[8,4,2,72,128]{4,3,2,1,0:T(8,128)(2,1)}), s16[8,4,2,72,128]{4,3,2,1,0:T(8,128)(2,1)S(1)}, u32[]{:S(2)}, u32[]{:S(2)}) async-start(s16[8,4,2,72,128]{4,3,2,1,0:T(8,128)(2,1)} %shard_map.68), calls=%async_computation | async-start | bytes 2359296 | tf_op jit(solution)/shard_map/all_to_all | solution.py:229
  11.1 0.0 copy-done
  11.1 0.1 copy.8
  11.2 0.1 reshape.29.targets
  11.3 16.9 %all-to-all-done = s16[8,4,2,72,128]{4,3,2,1,0:T(8,128)(2,1)S(1)} async-done(((s16[8,4,2,72,128]{4,3,2,1,0:T(8,128)(2,1)}), s16[8,4,2,72,128]{4,3,2,1,0:T(8,128)(2,1)S(1)}, u32[]{:S(2)}, u32[]{:S(2)}) %all-to-all-start) | async-done | bytes 1179680 | tf_op jit(solution)/shard_map/all_to_all | solution.py:229
  28.2 1.7 %shard_map.69 = (f32[32,72,128]{2,1,0:T(8,128)S(1)}, s16[32,72,128]{2,1,0:T(8,128)(2,1)S(1)}) custom-call(s32[64]{0:T(128)S(1)} %reshape.29.targets, s32[1]{0:T(128)} %bitcast.1.core, s16[64,72,128]{2,1,0:T(8,128)(2,1)S(1)} %bitcast.7), custom_call_target="tpu_custom_call" | custom-call | tf_op jit(solution)/shard_map/pallas_call | solution.py:230
  29.9 1.9 %collective-permute-start = (s16[32,72,128]{2,1,0:T(8,128)(2,1)S(1)}, s16[32,72,128]{2,1,0:T(8,128)(2,1)S(1)}, u32[]{:S(2)}, u32[]{:S(2)}) collective-permute-start(s16[32,72,128]{2,1,0:T(8,128)(2,1)S(1)} %get-tuple-element.9), channel_id=1, source_target_pairs={{0,8},{8,0},{1,9},{9,1},{2,10},{10,2},{3,11},{11,3},{4,12},{12,4},... | collective-permute-start | bytes 1769480 | tf_op jit(solution)/shard_map/ppermute | solution.py:236
  31.8 2.0 %collective-permute-done.got = s16[32,72,128]{2,1,0:T(8,128)(2,1)S(1)} collective-permute-done((s16[32,72,128]{2,1,0:T(8,128)(2,1)S(1)}, s16[32,72,128]{2,1,0:T(8,128)(2,1)S(1)}, u32[]{:S(2)}, u32[]{:S(2)}) %collective-permute-start) | collective-permute-done | bytes 589856 | tf_op jit(solution)/shard_map/ppermute | solution.py:236
  33.8 0.4 shard_map.70
  34.2 2.5 %collective-permute-start.1 = (s16[16,72,128]{2,1,0:T(8,128)(2,1)S(1)}, s16[16,72,128]{2,1,0:T(8,128)(2,1)S(1)}, u32[]{:S(2)}, u32[]{:S(2)}) collective-permute-start(s16[16,72,128]{2,1,0:T(8,128)(2,1)S(1)} %get-tuple-element.11), channel_id=1, source_target_pairs={{0,16},{16,0},{1,17},{17,1},{2,18},{18,2},{3,19},{19,3},{4,20},{20... | collective-permute-start | bytes 884744 | tf_op jit(solution)/shard_map/ppermute | solution.py:240
  36.8 9.9 %collective-permute-done.1.got = s16[16,72,128]{2,1,0:T(8,128)(2,1)S(1)} collective-permute-done((s16[16,72,128]{2,1,0:T(8,128)(2,1)S(1)}, s16[16,72,128]{2,1,0:T(8,128)(2,1)S(1)}, u32[]{:S(2)}, u32[]{:S(2)}) %collective-permute-start.1) | collective-permute-done | bytes 294944 | tf_op jit(solution)/shard_map/ppermute | solution.py:240
  46.7 0.3 shard_map.71
  47.0 34.5 %all_to_all.10.coded = s16[16,72,128]{2,1,0:T(8,128)(2,1)S(1)} all-to-all(s16[16,72,128]{2,1,0:T(8,128)(2,1)S(1)} %shard_map.71), channel_id=1, replica_groups=mesh['z'=16,'yh'=2,'core'=2,'coef'=8] {'z'}, dimensions={0} | all-to-all | bytes 589824 | tf_op jit(solution)/shard_map/all_to_all | solution.py:242
  81.4 0.9 %shard_map.72 = (f32[128,128]{1,0:T(8,128)}, f32[1,128]{1,0:T(1,128)}) custom-call(s16[16,72,128]{2,1,0:T(8,128)(2,1)S(1)} %all_to_all.10.coded), custom_call_target="tpu_custom_call" | custom-call | tf_op jit(solution)/shard_map/pallas_call | solution.py:243
Async XLA Ops:
  6.0 5.0 %copy-start = (s32[1,32,2]{1,2,0:T(2,128)S(1)}, s32[1,32,2]{1,2,0:T(2,128)}, u32[]{:S(2)}) copy-start(s32[1,32,2]{1,2,0:T(2,128)} %param.6) | copy-start | bytes 772
  6.1 22.1 %all-to-all-start = ((s16[8,4,2,72,128]{4,3,2,1,0:T(8,128)(2,1)}), s16[8,4,2,72,128]{4,3,2,1,0:T(8,128)(2,1)S(1)}, u32[]{:S(2)}, u32[]{:S(2)}) async-start(s16[8,4,2,72,128]{4,3,2,1,0:T(8,128)(2,1)} %shard_map.68), calls=%async_computation | async-start | bytes 2359296 | tf_op jit(solution)/shard_map/all_to_all | solution.py:229
  29.9 3.9 %collective-permute-start = (s16[32,72,128]{2,1,0:T(8,128)(2,1)S(1)}, s16[32,72,128]{2,1,0:T(8,128)(2,1)S(1)}, u32[]{:S(2)}, u32[]{:S(2)}) collective-permute-start(s16[32,72,128]{2,1,0:T(8,128)(2,1)S(1)} %get-tuple-element.9), channel_id=1, source_target_pairs={{0,8},{8,0},{1,9},{9,1},{2,10},{10,2},{3,11},{11,3},{4,12},{12,4},... | collective-permute-start | bytes 1769480 | tf_op jit(solution)/shard_map/ppermute | solution.py:236
  34.2 12.4 %collective-permute-start.1 = (s16[16,72,128]{2,1,0:T(8,128)(2,1)S(1)}, s16[16,72,128]{2,1,0:T(8,128)(2,1)S(1)}, u32[]{:S(2)}, u32[]{:S(2)}) collective-permute-start(s16[16,72,128]{2,1,0:T(8,128)(2,1)S(1)} %get-tuple-element.11), channel_id=1, source_target_pairs={{0,16},{16,0},{1,17},{17,1},{2,18},{18,2},{3,19},{19,3},{4,20},{20... | collective-permute-start | bytes 884744 | tf_op jit(solution)/shard_map/ppermute | solution.py:240

commit v4 on v3

--- a/solution.py
+++ b/solution.py
@@ -140,37 +140,37 @@
     loop(own.shape[0], unroll, split)
 
 
-def halve_kernel(unroll, part, own, got, kept, coded):
-    me = part[0]
-
-    def body(i):
-        mine, theirs = 2 * i + me, 2 * i + 1 - me
-        packed, diag, grad = decode(got[mine, :HALF], got[mine, HALF:])
-        kept[i, :HALF] = own[mine, :HALF] + packed
-        kept[i, HALF:] = own[mine, HALF:] + stack_rows([diag, grad])
-        packed, diag, grad = decode(got[theirs, :HALF], got[theirs, HALF:])
-        tail = own[theirs, HALF:]
-        coded[i, :HALF], coded[i, HALF:] = encode(own[theirs, :HALF] + packed, tail[0:1] + diag, tail[1:2] + grad)
-
-    loop(coded.shape[0], unroll, body)
-
-
-def recode_kernel(unroll, kept, got, coded):
+def join_kernel(unroll, own, got, coded):
+    near = coded.shape[0]
+
     def body(i):
         packed, diag, grad = decode(got[i, :HALF], got[i, HALF:])
-        tail = kept[i, HALF:]
-        coded[i, :HALF], coded[i, HALF:] = encode(kept[i, :HALF] + packed, tail[0:1] + diag, tail[1:2] + grad)
+        tail = own[i, HALF:]
+        main, tail = encode(own[i, :HALF] + packed, tail[0:1] + diag, tail[1:2] + grad)
+        to, slot = lax.rem(i, near), lax.div(i, near)
+        coded[to, slot, :HALF] = main
+        coded[to, slot, HALF:] = tail
+
+    loop(own.shape[0], unroll, body)
+
+
+def gather_sum(coded, i):
+    total = decode(coded[0, i, :HALF], coded[0, i, HALF:])
+    for k in range(1, coded.shape[0]):
+        more = decode(coded[k, i, :HALF], coded[k, i, HALF:])
+        total = [x + y for x, y in zip(total, more)]
+    return total
+
+
+def recode_kernel(unroll, got, coded):
+    def body(i):
+        coded[i, :HALF], coded[i, HALF:] = encode(*gather_sum(got, i))
 
     loop(coded.shape[0], unroll, body)
 
 
 def finish_kernel(coded, diag_out, grad_out):
-    packed = jnp.zeros((HALF, BS), jnp.float32)
-    diag = jnp.zeros((1, BS), jnp.float32)
-    grad = jnp.zeros((1, BS), jnp.float32)
-    for i in range(coded.shape[0]):
-        more = decode(coded[i, :HALF], coded[i, HALF:])
-        packed, diag, grad = packed + more[0], diag + more[1], grad + more[2]
+    packed, diag, grad = gather_sum(coded, 0)
     whole = jnp.concatenate([packed, pltpu.roll(packed, HALF, 1)], axis=0)
     flipped = whole.T
     r, c = iota((BS, BS), 0), iota((BS, BS), 1)
@@ -197,7 +197,8 @@
 
 def shards(jac_blocks, col_blocks, residual, run_of_half, run_scale):
     f32, i16 = jnp.float32, jnp.int16
-    slots = lax.axis_size("z") * 4
+    far = lax.axis_size("zq")
+    slots = far * 8
     n_rows, groups = jac_blocks.shape[:2]
     n_items = n_rows * groups * PAIR
 
@@ -234,12 +235,13 @@
         scratch=[pltpu.VMEM((slots, ROWS, BS), f32)],
     )(col_blocks.reshape(-1), index("core"), landed)
     got = lax.ppermute(other, "core", [(0, 1), (1, 0)])
-    kept, coded = call(
-        functools.partial(halve_kernel, 8), [shape(slots // 4, f32), shape(slots // 4, i16)], "svv"
-    )(index("yh"), own, got)
-    got = lax.ppermute(coded, "yh", [(0, 1), (1, 0)])
-    coded = call(functools.partial(recode_kernel, 8), shape(slots // 4, i16), "vv")(kept, got)
-    landed = lax.all_to_all(coded, "z", 0, 0, tiled=True)
+    near = slots // 2 // far
+    coded = call(
+        functools.partial(join_kernel, 8), jax.ShapeDtypeStruct((near, far, ROWS, BS), i16), "vv"
+    )(own, got)
+    landed = lax.all_to_all(coded, ("z0", "yh"), 0, 0, tiled=True)
+    coded = call(functools.partial(recode_kernel, 8), shape(far, i16), "v")(landed)
+    landed = lax.all_to_all(coded, "zq", 0, 0, tiled=True).reshape(far, 1, ROWS, BS)
     diag, grad = call(
         finish_kernel, [jax.ShapeDtypeStruct((BS, BS), f32), jax.ShapeDtypeStruct((1, BS), f32)], "v"
     )(landed)
@@ -247,8 +249,8 @@
 
 
 def solution(mesh):
-    fine = Mesh(mesh.devices.reshape(-1, 2, 2, mesh.devices.shape[1]), ("z", "yh", "core", "coef"))
-    batch = ("z", "yh", "core")
+    fine = Mesh(mesh.devices.reshape(-1, 2, 2, 2, mesh.devices.shape[1]), ("zq", "z0", "yh", "core", "coef"))
+    batch = ("zq", "z0", "yh", "core")
     in_specs = (
         P(batch + ("coef",), None, None, None, None),
         P("coef", batch, None),

time: 82.6 us -> 81.9 us (level)
  the two profiles are of different devices: /device:TPU:16 before, /device:TPU:2 now
where the time goes in v4:
time: 81.9 us; the launch traced here: 81.6 us
  blocking collectives  46.5 us (57%)
  waiting for transfers between devices  14.2 us (17%)
  starting transfers between devices  11.3 us (14%)
  Pallas kernels  8.75 us (11%)
    all_to_all x1, blocking collectives, shards(): lax.all_to_all(coded, 'zq', 0, 0, tiled=True).reshape(far, 1, ROWS, BS)  29.9 us
    all_to_all x1, blocking collectives, shards(): landed = lax.all_to_all(coded, ('z0', 'yh'), 0, 0, tiled=True)  16.5 us
    all_to_all x1, waiting for transfers between devices, shards(): lax.all_to_all(coded, 'coef', 0, 0, tiled=True).reshape(n_items, ROWS, BS)  12.2 us
    all_to_all x1, starting transfers between devices, shards(): lax.all_to_all(coded, 'coef', 0, 0, tiled=True).reshape(n_items, ROWS, BS)  9.39 us
    pallas_call x1, Pallas kernels, shards(): call(functools.partial(products_kernel, 8), jax.ShapeDtypeStruct((groups,...  5.38 us
    ppermute x1, waiting for transfers between devices, shards(): got = lax.ppermute(other, 'core', [(0, 1), (1, 0)])  1.97 us
    ppermute x1, starting transfers between devices, shards(): got = lax.ppermute(other, 'core', [(0, 1), (1, 0)])  1.92 us
    pallas_call x1, Pallas kernels, shards(): call(functools.partial(place_kernel, 8), [shape(slots // 2, f32), shape(s...  1.7 us
  transfers between devices with their start and end apart: 2, of which 2 were waited for; matrix products, arithmetic and copies ran while one was open for 0% of the time, Pallas kernels for 0%

profile of v4, /device:TPU:2, one launch (start us, length us, event | category | flops | bytes accessed | tf_op | source)
XLA Modules:
  0.0 81.6 jit_solution(5393987472672425119)
XLA Ops:
  0.6 5.4 %shard_map.68 = s16[8,4,2,72,128]{4,3,2,1,0:T(8,128)(2,1)} custom-call(s32[1]{0:T(128)} %bitcast.1.place, s32[64]{0:T(128)} %runs.1, bf16[32,128]{1,0:T(8,128)(2,1)} %bitcast.9, f32[32,128]{1,0:T(8,128)} %residual_hbm.1, bf16[4,8,2,128,128]{4,3,2,1,0:T(8,128)(2,1)} %jac_hbm.1), custom_call_target="tpu_custom_call" | custom-call | flops 268435456 | bytes 3145728 | tf_op jit(solution)/shard_map/pallas_call | solution.py:211
  6.0 0.0 copy-start
  6.0 9.4 %all-to-all-start = ((s16[8,4,2,72,128]{4,3,2,1,0:T(8,128)(2,1)}), s16[8,4,2,72,128]{4,3,2,1,0:T(8,128)(2,1)S(1)}, u32[]{:S(2)}, u32[]{:S(2)}) async-start(s16[8,4,2,72,128]{4,3,2,1,0:T(8,128)(2,1)} %shard_map.68), calls=%async_computation | async-start | bytes 2359296 | tf_op jit(solution)/shard_map/all_to_all | solution.py:230
  15.4 0.0 copy-done
  15.4 0.1 copy.8
  15.5 0.1 reshape.28.targets
  15.6 12.2 %all-to-all-done = s16[8,4,2,72,128]{4,3,2,1,0:T(8,128)(2,1)S(1)} async-done(((s16[8,4,2,72,128]{4,3,2,1,0:T(8,128)(2,1)}), s16[8,4,2,72,128]{4,3,2,1,0:T(8,128)(2,1)S(1)}, u32[]{:S(2)}, u32[]{:S(2)}) %all-to-all-start) | async-done | bytes 1179680 | tf_op jit(solution)/shard_map/all_to_all | solution.py:230
  27.8 1.7 %shard_map.69 = (f32[32,72,128]{2,1,0:T(8,128)S(1)}, s16[32,72,128]{2,1,0:T(8,128)(2,1)S(1)}) custom-call(s32[64]{0:T(128)S(1)} %reshape.28.targets, s32[1]{0:T(128)} %bitcast.core, s16[64,72,128]{2,1,0:T(8,128)(2,1)S(1)} %bitcast.7), custom_call_target="tpu_custom_call" | custom-call | tf_op jit(solution)/shard_map/pallas_call | solution.py:231
  29.5 1.9 %collective-permute-start = (s16[32,72,128]{2,1,0:T(8,128)(2,1)S(1)}, s16[32,72,128]{2,1,0:T(8,128)(2,1)S(1)}, u32[]{:S(2)}, u32[]{:S(2)}) collective-permute-start(s16[32,72,128]{2,1,0:T(8,128)(2,1)S(1)} %get-tuple-element.7), channel_id=1, source_target_pairs={{0,8},{8,0},{1,9},{9,1},{2,10},{10,2},{3,11},{11,3},{4,12},{12,4},... | collective-permute-start | bytes 1769480 | tf_op jit(solution)/shard_map/ppermute | solution.py:237
  31.5 2.0 %collective-permute-done.got = s16[32,72,128]{2,1,0:T(8,128)(2,1)S(1)} collective-permute-done((s16[32,72,128]{2,1,0:T(8,128)(2,1)S(1)}, s16[32,72,128]{2,1,0:T(8,128)(2,1)S(1)}, u32[]{:S(2)}, u32[]{:S(2)}) %collective-permute-start) | collective-permute-done | bytes 589856 | tf_op jit(solution)/shard_map/ppermute | solution.py:237
  33.4 0.6 shard_map.70
  34.0 16.5 %all_to_all.15.got = s16[4,8,72,128]{3,2,1,0:T(8,128)(2,1)S(1)} all-to-all(s16[4,8,72,128]{3,2,1,0:T(8,128)(2,1)S(1)} %shard_map.70), channel_id=1, replica_groups=mesh['zq'=8,'z0'=2,'yh'=2,'core'=2,'coef'=8] {'z0','yh'}, dimensions={0} | all-to-all | bytes 1179648 | tf_op jit(solution)/shard_map/all_to_all | solution.py:242
  50.5 0.3 shard_map.71
  50.8 29.9 %all_to_all.16 = s16[8,72,128]{2,1,0:T(8,128)(2,1)S(1)} all-to-all(s16[8,72,128]{2,1,0:T(8,128)(2,1)S(1)} %shard_map.71), channel_id=1, replica_groups=mesh['zq'=8,'z0'=2,'yh'=2,'core'=2,'coef'=8] {'zq'}, dimensions={0} | all-to-all | bytes 294912 | tf_op jit(solution)/shard_map/all_to_all | solution.py:244
  80.8 0.8 shard_map.72
Async XLA Ops:
  6.0 9.4 %copy-start = (s32[1,32,2]{1,2,0:T(2,128)S(1)}, s32[1,32,2]{1,2,0:T(2,128)}, u32[]{:S(2)}) copy-start(s32[1,32,2]{1,2,0:T(2,128)} %param.6) | copy-start | bytes 772
  6.0 21.8 %all-to-all-start = ((s16[8,4,2,72,128]{4,3,2,1,0:T(8,128)(2,1)}), s16[8,4,2,72,128]{4,3,2,1,0:T(8,128)(2,1)S(1)}, u32[]{:S(2)}, u32[]{:S(2)}) async-start(s16[8,4,2,72,128]{4,3,2,1,0:T(8,128)(2,1)} %shard_map.68), calls=%async_computation | async-start | bytes 2359296 | tf_op jit(solution)/shard_map/all_to_all | solution.py:230
  29.5 3.9 %collective-permute-start = (s16[32,72,128]{2,1,0:T(8,128)(2,1)S(1)}, s16[32,72,128]{2,1,0:T(8,128)(2,1)S(1)}, u32[]{:S(2)}, u32[]{:S(2)}) collective-permute-start(s16[32,72,128]{2,1,0:T(8,128)(2,1)S(1)} %get-tuple-element.7), channel_id=1, source_target_pairs={{0,8},{8,0},{1,9},{9,1},{2,10},{10,2},{3,11},{11,3},{4,12},{12,4},... | collective-permute-start | bytes 1769480 | tf_op jit(solution)/shard_map/ppermute | solution.py:237

commit v5 on v4

--- a/solution.py
+++ b/solution.py
@@ -67,91 +67,96 @@
     return packed, tail[0:1] * scale, (tail[3:4] + tail[4:5] * (1.0 / FULL)) * scale_g
 
 
-def products_kernel(unroll, place, runs, scales_hbm, residual_hbm, jac_hbm, out_hbm, jac, coded, scales, residual, table, sem, out_sem, aux_sem):
+def products_kernel(unroll, runs_hbm, scales_hbm, residual_hbm, jac_hbm, coded, jac, runs, scales, residual, table, sem, aux_sem):
     n_rows, groups = jac_hbm.shape[:2]
+    aux = [
+        pltpu.make_async_copy(runs_hbm, runs, aux_sem.at[0]),
+        pltpu.make_async_copy(scales_hbm, scales, aux_sem.at[1]),
+        pltpu.make_async_copy(residual_hbm, residual, aux_sem.at[2]),
+    ]
     copies = [pltpu.make_async_copy(jac_hbm.at[r], jac.at[r], sem.at[r]) for r in range(n_rows)]
-    aux = [
-        pltpu.make_async_copy(scales_hbm, scales, aux_sem.at[0]),
-        pltpu.make_async_copy(residual_hbm, residual, aux_sem.at[1]),
-    ]
     for copy in aux + copies:
         copy.start()
-    done = []
+    first = lax.axis_index("coef") * n_rows
+    upper = iota((HALF, BS), 1) >= iota((HALF, BS), 0)
+    lanes = iota((HALF, BS), 1) == iota((HALF, BS), 0)
+    lane = iota((1, BS), 1)
     for copy in aux:
         copy.wait()
     table[...] = scales[...].astype(jnp.float32)
-    upper = iota((HALF, BS), 1) >= iota((HALF, BS), 0)
-    lanes = iota((HALF, BS), 1) == iota((HALF, BS), 0)
-    lane = iota((1, BS), 1)
 
     def scale(half):
         run = runs[half]
         line = table[pl.ds(lax.div(run, BS), 1), :]
         return jnp.sum(jnp.where(lane == lax.rem(run, BS), line, 0.0), axis=1, keepdims=True)
 
+    weights, terms = [], []
     for r in range(n_rows):
-        row = place[0] * n_rows + r
+        row = first + r
         w = jnp.where(lane < HALF, scale(2 * row), scale(2 * row + 1))
         wr = w * residual[pl.ds(row, 1), :]
         hi = wr.astype(jnp.bfloat16).astype(jnp.float32)
         mid = (wr - hi).astype(jnp.bfloat16).astype(jnp.float32)
-        terms = stack_rows([hi, mid, wr - hi - mid])
-        terms = jnp.concatenate([terms, jnp.zeros_like(terms)], axis=0).astype(jnp.bfloat16)
+        split = stack_rows([hi, mid, wr - hi - mid])
+        weights.append(w)
+        terms.append(jnp.concatenate([split, jnp.zeros_like(split)], axis=0).astype(jnp.bfloat16))
+
+    for r in range(n_rows):
         copies[r].wait()
 
         def body(g):
             for s in range(PAIR):
                 one = jac[r, g, s]
-                scaled = (one.T.astype(jnp.float32) * w).astype(jnp.bfloat16)
-                left = jnp.concatenate([scaled, terms], axis=0)
+                scaled = (one.T.astype(jnp.float32) * weights[r]).astype(jnp.bfloat16)
+                left = jnp.concatenate([scaled, terms[r]], axis=0)
                 out = lax.dot_general(left, one, (((1,), (0,)), ((), ())), preferred_element_type=jnp.float32)
                 last = pltpu.roll(out[HALF:BS], HALF, 1)
                 packed = jnp.where(upper, out[:HALF], last)
                 diag = jnp.sum(jnp.where(lanes, last, 0.0), axis=0, keepdims=True)
                 grad = jnp.sum(out[BS : BS + 8], axis=0, keepdims=True)
                 main, tail = encode(packed, diag, grad)
-                coded[r, g, s, :HALF] = main
-                coded[r, g, s, HALF:] = tail
+                coded[g, r, s, :HALF] = main
+                coded[g, r, s, HALF:] = tail
 
         loop(groups, unroll, body)
-        done.append(pltpu.make_async_copy(coded.at[r], out_hbm.at[:, r], out_sem.at[r]))
-        done[-1].start()
-    for copy in done:
-        copy.wait()
-
-
-def place_kernel(unroll, targets, core, coded, own, other, acc):
+
+
+def place_kernel(unroll, targets_hbm, coded, acc, other, targets, sem):
+    copy = pltpu.make_async_copy(targets_hbm, targets, sem)
+    copy.start()
     acc[...] = jnp.zeros_like(acc)
+    copy.wait()
 
     def body(i):
         packed, diag, grad = decode(coded[i, :HALF], coded[i, HALF:])
-        where = targets[i]
+        where = targets[lax.rem(i, PAIR), lax.div(i, PAIR)]
         acc[where, :HALF] += packed
         acc[where, HALF:] += stack_rows([diag, grad])
 
     loop(coded.shape[0], unroll, body)
-    me = core[0]
+    theirs = 1 - lax.axis_index("core")
 
     def split(i):
-        own[i] = acc[2 * i + me]
-        value = acc[2 * i + 1 - me]
+        value = acc[2 * i + theirs]
         other[i, :HALF], other[i, HALF:] = encode(value[:HALF], value[HALF : HALF + 1], value[HALF + 1 : HALF + 2])
 
-    loop(own.shape[0], unroll, split)
-
-
-def join_kernel(unroll, own, got, coded):
+    loop(other.shape[0], unroll, split)
+
+
+def join_kernel(unroll, acc, got, coded):
     near = coded.shape[0]
+    me = lax.axis_index("core")
 
     def body(i):
         packed, diag, grad = decode(got[i, :HALF], got[i, HALF:])
-        tail = own[i, HALF:]
-        main, tail = encode(own[i, :HALF] + packed, tail[0:1] + diag, tail[1:2] + grad)
+        mine = 2 * i + me
+        tail = acc[mine, HALF:]
+        main, tail = encode(acc[mine, :HALF] + packed, tail[0:1] + diag, tail[1:2] + grad)
         to, slot = lax.rem(i, near), lax.div(i, near)
         coded[to, slot, :HALF] = main
         coded[to, slot, HALF:] = tail
 
-    loop(own.shape[0], unroll, body)
+    loop(got.shape[0], unroll, body)
 
 
 def gather_sum(coded, i):
@@ -202,43 +207,39 @@
     n_rows, groups = jac_blocks.shape[:2]
     n_items = n_rows * groups * PAIR
 
-    def index(name):
-        return lax.axis_index(name).astype(jnp.int32).reshape(1)
-
     def shape(n, dtype):
         return jax.ShapeDtypeStruct((n, ROWS, BS), dtype)
 
+    targets = col_blocks[0].T
     coded = call(
         functools.partial(products_kernel, 8),
         jax.ShapeDtypeStruct((groups, n_rows, PAIR, ROWS, BS), i16),
-        "sshhh",
-        out="h",
+        "hhhh",
         vmem=60,
         scratch=[
             pltpu.VMEM(jac_blocks.shape, jnp.bfloat16),
-            pltpu.VMEM((n_rows, groups, PAIR, ROWS, BS), i16),
+            pltpu.SMEM(run_of_half.shape, jnp.int32),
             pltpu.VMEM((run_scale.shape[0] // BS, BS), jnp.bfloat16),
             pltpu.VMEM(residual.shape, f32),
             pltpu.VMEM((run_scale.shape[0] // BS, BS), f32),
             pltpu.SemaphoreType.DMA((n_rows,)),
-            pltpu.SemaphoreType.DMA((n_rows,)),
-            pltpu.SemaphoreType.DMA((2,)),
+            pltpu.SemaphoreType.DMA((3,)),
         ],
         flops=2 * n_items * BS**3,
         moved=n_items * BS * BS * 3,
-    )(index("coef"), run_of_half, run_scale.reshape(-1, BS), residual, jac_blocks)
+    )(run_of_half, run_scale.reshape(-1, BS), residual, jac_blocks)
     landed = lax.all_to_all(coded, "coef", 0, 0, tiled=True).reshape(n_items, ROWS, BS)
-    own, other = call(
+    acc, other = call(
         functools.partial(place_kernel, 8),
-        [shape(slots // 2, f32), shape(slots // 2, i16)],
-        "ssv",
-        scratch=[pltpu.VMEM((slots, ROWS, BS), f32)],
-    )(col_blocks.reshape(-1), index("core"), landed)
+        [shape(slots, f32), shape(slots // 2, i16)],
+        "hv",
+        scratch=[pltpu.SMEM(targets.shape, jnp.int32), pltpu.SemaphoreType.DMA],
+    )(targets, landed)
     got = lax.ppermute(other, "core", [(0, 1), (1, 0)])
     near = slots // 2 // far
     coded = call(
         functools.partial(join_kernel, 8), jax.ShapeDtypeStruct((near, far, ROWS, BS), i16), "vv"
-    )(own, got)
+    )(acc, got)
     landed = lax.all_to_all(coded, ("z0", "yh"), 0, 0, tiled=True)
     coded = call(functools.partial(recode_kernel, 8), shape(far, i16), "v")(landed)
     landed = lax.all_to_all(coded, "zq", 0, 0, tiled=True).reshape(far, 1, ROWS, BS)

time: 81.9 us -> 81.4 us (level)
  the two profiles are of different devices: /device:TPU:2 before, /device:TPU:6 now
where the time goes in v5:
time: 81.4 us; the launch traced here: 80.3 us
  blocking collectives  67.5 us (83%)
  Pallas kernels  8.16 us (10%)
  waiting for transfers between devices  1.97 us (2%)
  starting transfers between devices  1.92 us (2%)
    all_to_all x1, blocking collectives, shards(): lax.all_to_all(coded, 'zq', 0, 0, tiled=True).reshape(far, 1, ROWS, BS)  29.9 us
    all_to_all x1, blocking collectives, shards(): lax.all_to_all(coded, 'coef', 0, 0, tiled=True).reshape(n_items, ROWS, BS)  21 us
    all_to_all x1, blocking collectives, shards(): landed = lax.all_to_all(coded, ('z0', 'yh'), 0, 0, tiled=True)  16.7 us
    pallas_call x1, Pallas kernels, shards(): call(functools.partial(products_kernel, 8), jax.ShapeDtypeStruct((groups,...  5.01 us
    ppermute x1, waiting for transfers between devices, shards(): got = lax.ppermute(other, 'core', [(0, 1), (1, 0)])  1.97 us
    ppermute x1, starting transfers between devices, shards(): got = lax.ppermute(other, 'core', [(0, 1), (1, 0)])  1.92 us
  transfers between devices with their start and end apart: 1, of which 1 were waited for; matrix products, arithmetic and copies ran while one was open for 0% of the time, Pallas kernels for 0%

profile of v5, /device:TPU:6, one launch (start us, length us, event | category | flops | bytes accessed | tf_op | source)
XLA Modules:
  0.0 80.3 jit_solution(9677064344569262090)
XLA Ops:
  0.6 0.0 copy-start
  0.6 5.0 %shard_map.68 = s16[8,4,2,72,128]{4,3,2,1,0:T(8,128)(2,1)} custom-call(s32[64]{0:T(128)} %runs_hbm.1, bf16[32,128]{1,0:T(8,128)(2,1)} %bitcast.11, f32[32,128]{1,0:T(8,128)} %residual_hbm.1, bf16[4,8,2,128,128]{4,3,2,1,0:T(8,128)(2,1)} %jac_hbm.1), custom_call_target="tpu_custom_call" | custom-call | flops 268435456 | bytes 3145728 | tf_op jit(solution)/shard_map/pallas_call | solution.py:214
  5.7 21.0 %all_to_all.15 = s16[8,4,2,72,128]{4,3,2,1,0:T(8,128)(2,1)S(1)} all-to-all(s16[8,4,2,72,128]{4,3,2,1,0:T(8,128)(2,1)} %shard_map.68), channel_id=1, replica_groups=mesh['zq'=8,'z0'=2,'yh'=2,'core'=2,'coef'=8] {'coef'}, dimensions={0} | all-to-all | bytes 2359296 | tf_op jit(solution)/shard_map/all_to_all | solution.py:231
  26.6 0.0 copy-done
  26.6 1.5 %shard_map.69 = (f32[64,72,128]{2,1,0:T(8,128)S(1)}, s16[32,72,128]{2,1,0:T(8,128)(2,1)S(1)}) custom-call(s32[2,32]{1,0:T(2,128)S(1)} %bitcast.10, s16[64,72,128]{2,1,0:T(8,128)(2,1)S(1)} %bitcast.8), custom_call_target="tpu_custom_call" | custom-call | tf_op jit(solution)/shard_map/pallas_call | solution.py:232
  28.1 1.9 %collective-permute-start = (s16[32,72,128]{2,1,0:T(8,128)(2,1)S(1)}, s16[32,72,128]{2,1,0:T(8,128)(2,1)S(1)}, u32[]{:S(2)}, u32[]{:S(2)}) collective-permute-start(s16[32,72,128]{2,1,0:T(8,128)(2,1)S(1)} %get-tuple-element.7), channel_id=1, source_target_pairs={{0,8},{8,0},{1,9},{9,1},{2,10},{10,2},{3,11},{11,3},{4,12},{12,4},... | collective-permute-start | bytes 1769480 | tf_op jit(solution)/shard_map/ppermute | solution.py:238
  30.0 2.0 %collective-permute-done.got = s16[32,72,128]{2,1,0:T(8,128)(2,1)S(1)} collective-permute-done((s16[32,72,128]{2,1,0:T(8,128)(2,1)S(1)}, s16[32,72,128]{2,1,0:T(8,128)(2,1)S(1)}, u32[]{:S(2)}, u32[]{:S(2)}) %collective-permute-start) | collective-permute-done | bytes 589856 | tf_op jit(solution)/shard_map/ppermute | solution.py:238
  32.0 0.6 shard_map.70
  32.6 16.7 %all_to_all.16.got = s16[4,8,72,128]{3,2,1,0:T(8,128)(2,1)S(1)} all-to-all(s16[4,8,72,128]{3,2,1,0:T(8,128)(2,1)S(1)} %shard_map.70), channel_id=1, replica_groups=mesh['zq'=8,'z0'=2,'yh'=2,'core'=2,'coef'=8] {'z0','yh'}, dimensions={0} | all-to-all | bytes 1179648 | tf_op jit(solution)/shard_map/all_to_all | solution.py:243
  49.2 0.3 shard_map.71
  49.5 29.9 %all_to_all.17 = s16[8,72,128]{2,1,0:T(8,128)(2,1)S(1)} all-to-all(s16[8,72,128]{2,1,0:T(8,128)(2,1)S(1)} %shard_map.71), channel_id=1, replica_groups=mesh['zq'=8,'z0'=2,'yh'=2,'core'=2,'coef'=8] {'zq'}, dimensions={0} | all-to-all | bytes 294912 | tf_op jit(solution)/shard_map/all_to_all | solution.py:245
  79.4 0.8 %shard_map.72 = (f32[128,128]{1,0:T(8,128)}, f32[1,128]{1,0:T(1,128)}) custom-call(s16[8,1,72,128]{3,2,1,0:T(8,128)(2,1)S(1)} %bitcast.9), custom_call_target="tpu_custom_call" | custom-call | tf_op jit(solution)/shard_map/pallas_call | solution.py:246
Async XLA Ops:
  0.6 26.0 %copy-start = (s32[1,32,2]{1,2,0:T(2,128)S(1)}, s32[1,32,2]{1,2,0:T(2,128)}, u32[]{:S(2)}) copy-start(s32[1,32,2]{1,2,0:T(2,128)} %param.6) | copy-start | bytes 772
  28.1 3.9 %collective-permute-start = (s16[32,72,128]{2,1,0:T(8,128)(2,1)S(1)}, s16[32,72,128]{2,1,0:T(8,128)(2,1)S(1)}, u32[]{:S(2)}, u32[]{:S(2)}) collective-permute-start(s16[32,72,128]{2,1,0:T(8,128)(2,1)S(1)} %get-tuple-element.7), channel_id=1, source_target_pairs={{0,8},{8,0},{1,9},{9,1},{2,10},{10,2},{3,11},{11,3},{4,12},{12,4},... | collective-permute-start | bytes 1769480 | tf_op jit(solution)/shard_map/ppermute | solution.py:238

commit v6 on v5

--- a/solution.py
+++ b/solution.py
@@ -13,6 +13,7 @@
 HALF = BS // 2
 PAIR = 2
 ROWS = HALF + 8
+DUO = 2 * HALF + 8
 FULL = 32000.0
 STEPS = 16.0
 TINY = 1e-30
@@ -48,7 +49,7 @@
 
 def encode(packed, diag, grad):
     big = jnp.maximum(jnp.max(jnp.abs(packed), axis=0, keepdims=True), jnp.maximum(jnp.abs(diag), TINY))
-    big_g = jnp.maximum(jnp.abs(grad), TINY)
+    big_g = jnp.maximum(jnp.maximum(jnp.abs(grad), pltpu.roll(jnp.abs(grad), HALF, 1)), TINY)
     code = jnp.ceil(jnp.log(big) * PER)
     code_g = jnp.ceil(jnp.log(big_g) * PER)
     inv = jnp.exp2(code * (-1.0 / STEPS)) * FULL
@@ -56,15 +57,28 @@
     g = grad * inv_g
     g_hi = jnp.round(g)
     g_lo = (g - g_hi) * FULL
-    return to_int16(packed * inv), to_int16(stack_rows([diag * inv, code, code_g, g_hi, g_lo]))
+    first = jnp.where(iota((1, BS), 1) < HALF, diag * inv, code_g)
+    return packed * inv, [first, code, g_hi, g_lo]
+
+
+def put_two(coded, at, two):
+    for k, (main, _) in enumerate(two):
+        coded[at + (pl.ds(k * HALF, HALF),)] = to_int16(main)
+    coded[at + (pl.ds(2 * HALF, 8),)] = to_int16(stack_rows(two[0][1] + two[1][1]))
 
 
 def decode(main, tail):
-    tail = tail.astype(jnp.int32).astype(jnp.float32)
+    low = iota((1, BS), 1) < HALF
+    code_g = jnp.where(low, pltpu.roll(tail[0:1], HALF, 1), tail[0:1])
     scale = jnp.exp2(tail[1:2] * (1.0 / STEPS)) * (1.0 / FULL)
-    scale_g = jnp.exp2(tail[2:3] * (1.0 / STEPS)) * (1.0 / FULL)
+    scale_g = jnp.exp2(code_g * (1.0 / STEPS)) * (1.0 / FULL)
     packed = main.astype(jnp.int32).astype(jnp.float32) * scale
-    return packed, tail[0:1] * scale, (tail[3:4] + tail[4:5] * (1.0 / FULL)) * scale_g
+    return packed, jnp.where(low, tail[0:1] * scale, 0.0), (tail[2:3] + tail[3:4] * (1.0 / FULL)) * scale_g
+
+
+def get_two(coded, at):
+    tail = coded[at + (pl.ds(2 * HALF, 8),)].astype(jnp.int32).astype(jnp.float32)
+    return [decode(coded[at + (pl.ds(k * HALF, HALF),)], tail[4 * k : 4 * k + 4]) for k in range(2)]
 
 
 def products_kernel(unroll, runs_hbm, scales_hbm, residual_hbm, jac_hbm, coded, jac, runs, scales, residual, table, sem, aux_sem):
@@ -98,25 +112,25 @@
         hi = wr.astype(jnp.bfloat16).astype(jnp.float32)
         mid = (wr - hi).astype(jnp.bfloat16).astype(jnp.float32)
         split = stack_rows([hi, mid, wr - hi - mid])
-        weights.append(w)
+        weights.append(jnp.broadcast_to(w, (BS, BS)).astype(jnp.bfloat16))
         terms.append(jnp.concatenate([split, jnp.zeros_like(split)], axis=0).astype(jnp.bfloat16))
 
     for r in range(n_rows):
         copies[r].wait()
 
         def body(g):
+            two = []
             for s in range(PAIR):
                 one = jac[r, g, s]
-                scaled = (one.T.astype(jnp.float32) * weights[r]).astype(jnp.bfloat16)
+                scaled = one.T * weights[r]
                 left = jnp.concatenate([scaled, terms[r]], axis=0)
                 out = lax.dot_general(left, one, (((1,), (0,)), ((), ())), preferred_element_type=jnp.float32)
                 last = pltpu.roll(out[HALF:BS], HALF, 1)
                 packed = jnp.where(upper, out[:HALF], last)
                 diag = jnp.sum(jnp.where(lanes, last, 0.0), axis=0, keepdims=True)
                 grad = jnp.sum(out[BS : BS + 8], axis=0, keepdims=True)
-                main, tail = encode(packed, diag, grad)
-                coded[g, r, s, :HALF] = main
-                coded[g, r, s, HALF:] = tail
+                two.append(encode(packed, diag, grad))
+            put_two(coded, (g, r), two)
 
         loop(groups, unroll, body)
 
@@ -127,55 +141,65 @@
     acc[...] = jnp.zeros_like(acc)
     copy.wait()
 
-    def body(i):
-        packed, diag, grad = decode(coded[i, :HALF], coded[i, HALF:])
-        where = targets[lax.rem(i, PAIR), lax.div(i, PAIR)]
-        acc[where, :HALF] += packed
-        acc[where, HALF:] += stack_rows([diag, grad])
+    def body(row):
+        for s, (packed, diag, grad) in enumerate(get_two(coded, (row,))):
+            where = targets[s, row]
+            acc[where, :HALF] += packed
+            acc[where, HALF:] += stack_rows([diag, grad])
 
     loop(coded.shape[0], unroll, body)
     theirs = 1 - lax.axis_index("core")
 
     def split(i):
-        value = acc[2 * i + theirs]
-        other[i, :HALF], other[i, HALF:] = encode(value[:HALF], value[HALF : HALF + 1], value[HALF + 1 : HALF + 2])
+        put_two(other, (i,), [encode_slot(acc[2 * (2 * i + k) + theirs]) for k in range(2)])
 
     loop(other.shape[0], unroll, split)
 
 
+def encode_slot(value):
+    return encode(value[:HALF], value[HALF : HALF + 1], value[HALF + 1 : HALF + 2])
+
+
 def join_kernel(unroll, acc, got, coded):
-    near = coded.shape[0]
     me = lax.axis_index("core")
 
     def body(i):
-        packed, diag, grad = decode(got[i, :HALF], got[i, HALF:])
-        mine = 2 * i + me
-        tail = acc[mine, HALF:]
-        main, tail = encode(acc[mine, :HALF] + packed, tail[0:1] + diag, tail[1:2] + grad)
-        to, slot = lax.rem(i, near), lax.div(i, near)
-        coded[to, slot, :HALF] = main
-        coded[to, slot, HALF:] = tail
-
-    loop(got.shape[0], unroll, body)
-
-
-def gather_sum(coded, i):
-    total = decode(coded[0, i, :HALF], coded[0, i, HALF:])
-    for k in range(1, coded.shape[0]):
-        more = decode(coded[k, i, :HALF], coded[k, i, HALF:])
+        far, bit = lax.div(i, 2), lax.rem(i, 2)
+        new = ([], [])
+        for k in range(2):
+            at = 4 * far + 2 * k + bit
+            for y, more in enumerate(get_two(got, (at,))):
+                mine = acc[2 * (2 * at + y) + me]
+                parts = mine[:HALF], mine[HALF : HALF + 1], mine[HALF + 1 : HALF + 2]
+                new[y].append(encode(*[p + q for p, q in zip(parts, more)]))
+        for y in range(2):
+            put_two(coded, (2 * bit + y, far), new[y])
+
+    loop(got.shape[0] // 2, unroll, body)
+
+
+def add_up(several):
+    total = several[0]
+    for more in several[1:]:
         total = [x + y for x, y in zip(total, more)]
     return total
 
 
 def recode_kernel(unroll, got, coded):
     def body(i):
-        coded[i, :HALF], coded[i, HALF:] = encode(*gather_sum(got, i))
-
-    loop(coded.shape[0], unroll, body)
+        several = [get_two(got, (k, i)) for k in range(got.shape[0])]
+        for k in range(2):
+            main, tail = encode(*add_up([two[k] for two in several]))
+            coded[2 * i + k, :HALF] = to_int16(main)
+            coded[2 * i + k, HALF:] = to_int16(stack_rows(tail))
+
+    loop(got.shape[1], unroll, body)
 
 
 def finish_kernel(coded, diag_out, grad_out):
-    packed, diag, grad = gather_sum(coded, 0)
+    packed, diag, grad = add_up(
+        [decode(coded[k, :HALF], coded[k, HALF:].astype(jnp.int32).astype(jnp.float32)) for k in range(coded.shape[0])]
+    )
     whole = jnp.concatenate([packed, pltpu.roll(packed, HALF, 1)], axis=0)
     flipped = whole.T
     r, c = iota((BS, BS), 0), iota((BS, BS), 1)
@@ -213,9 +237,9 @@
     targets = col_blocks[0].T
     coded = call(
         functools.partial(products_kernel, 8),
-        jax.ShapeDtypeStruct((groups, n_rows, PAIR, ROWS, BS), i16),
+        jax.ShapeDtypeStruct((groups, n_rows, DUO, BS), i16),
         "hhhh",
-        vmem=60,
+        vmem=32,
         scratch=[
             pltpu.VMEM(jac_blocks.shape, jnp.bfloat16),
             pltpu.SMEM(run_of_half.shape, jnp.int32),
@@ -227,22 +251,22 @@
         ],
         flops=2 * n_items * BS**3,
         moved=n_items * BS * BS * 3,
-    )(run_of_half, run_scale.reshape(-1, BS), residual, jac_blocks)
-    landed = lax.all_to_all(coded, "coef", 0, 0, tiled=True).reshape(n_items, ROWS, BS)
+    )(*[pltpu.with_memory_space_constraint(x, pltpu.HBM) for x in (run_of_half, run_scale.reshape(-1, BS), residual, jac_blocks)])
+    landed = lax.all_to_all(coded, "coef", 0, 0, tiled=True).reshape(n_items // PAIR, DUO, BS)
     acc, other = call(
-        functools.partial(place_kernel, 8),
-        [shape(slots, f32), shape(slots // 2, i16)],
+        functools.partial(place_kernel, 16),
+        [shape(slots, f32), jax.ShapeDtypeStruct((slots // 4, DUO, BS), i16)],
         "hv",
         scratch=[pltpu.SMEM(targets.shape, jnp.int32), pltpu.SemaphoreType.DMA],
     )(targets, landed)
     got = lax.ppermute(other, "core", [(0, 1), (1, 0)])
     near = slots // 2 // far
     coded = call(
-        functools.partial(join_kernel, 8), jax.ShapeDtypeStruct((near, far, ROWS, BS), i16), "vv"
+        functools.partial(join_kernel, 16), jax.ShapeDtypeStruct((near, far // 2, DUO, BS), i16), "vv"
     )(acc, got)
     landed = lax.all_to_all(coded, ("z0", "yh"), 0, 0, tiled=True)
     coded = call(functools.partial(recode_kernel, 8), shape(far, i16), "v")(landed)
-    landed = lax.all_to_all(coded, "zq", 0, 0, tiled=True).reshape(far, 1, ROWS, BS)
+    landed = lax.all_to_all(coded, "zq", 0, 0, tiled=True)
     diag, grad = call(
         finish_kernel, [jax.ShapeDtypeStruct((BS, BS), f32), jax.ShapeDtypeStruct((1, BS), f32)], "v"
     )(landed)

time: 81.4 us -> 79.4 us (0.975)
  blocking collectives: 67.5 us -> 66.5 us
  Pallas kernels: 8.16 us -> 7.33 us
    pallas_call x1, Pallas kernels: 5.01 us -> 4.05 us  [shards(): call(functools.partial(products_kernel, 8), jax.ShapeDtypeStruct((groups,...]
where the time goes in v6:
time: 79.4 us; the launch traced here: 78.4 us
  blocking collectives  66.5 us (84%)
  Pallas kernels  7.33 us (9%)
  starting transfers between devices  1.92 us (2%)
  waiting for transfers between devices  1.92 us (2%)
    all_to_all x1, blocking collectives, shards(): landed = lax.all_to_all(coded, 'zq', 0, 0, tiled=True)  30 us
    all_to_all x1, blocking collectives, shards(): lax.all_to_all(coded, 'coef', 0, 0, tiled=True)  20.2 us
    all_to_all x1, blocking collectives, shards(): landed = lax.all_to_all(coded, ('z0', 'yh'), 0, 0, tiled=True)  16.3 us
    pallas_call x1, Pallas kernels, shards(): call(functools.partial(products_kernel, 8), jax.ShapeDtypeStruct((groups,...  4.05 us
    ppermute x1, waiting for transfers between devices, shards(): got = lax.ppermute(other, 'core', [(0, 1), (1, 0)])  1.92 us
    ppermute x1, starting transfers between devices, shards(): got = lax.ppermute(other, 'core', [(0, 1), (1, 0)])  1.92 us
  transfers between devices with their start and end apart: 1, of which 1 were waited for; matrix products, arithmetic and copies ran while one was open for 0% of the time, Pallas kernels for 0%

profile of v6, /device:TPU:6, one launch (start us, length us, event | category | flops | bytes accessed | tf_op | source)
XLA Modules:
  0.0 78.4 jit_solution(5903878758094938494)
XLA Ops:
  0.6 0.0 copy-start
  0.6 4.0 %shard_map.68 = s16[8,4,136,128]{3,2,1,0:T(8,128)(2,1)S(1)} custom-call(s32[64]{0:T(128)} %runs_hbm.1, bf16[32,128]{1,0:T(8,128)(2,1)} %bitcast.9, f32[32,128]{1,0:T(8,128)} %residual_hbm.1, bf16[4,8,2,128,128]{4,3,2,1,0:T(8,128)(2,1)} %jac_hbm.1), custom_call_target="tpu_custom_call" | custom-call | flops 268435456 | bytes 3145728 | tf_op jit(solution)/shard_map/pallas_call | solution.py:238
  4.7 20.2 %all_to_all.15 = s16[8,4,136,128]{3,2,1,0:T(8,128)(2,1)S(1)} all-to-all(s16[8,4,136,128]{3,2,1,0:T(8,128)(2,1)S(1)} %shard_map.68), channel_id=1, replica_groups=mesh['zq'=8,'z0'=2,'yh'=2,'core'=2,'coef'=8] {'coef'}, dimensions={0} | all-to-all | bytes 2228224 | tf_op jit(solution)/shard_map/all_to_all | solution.py:255
  24.9 0.0 copy-done
  24.9 1.5 %shard_map.69 = (f32[64,72,128]{2,1,0:T(8,128)S(1)}, s16[16,136,128]{2,1,0:T(8,128)(2,1)S(1)}) custom-call(s32[2,32]{1,0:T(2,128)S(1)} %bitcast.8, s16[32,136,128]{2,1,0:T(8,128)(2,1)S(1)} %bitcast.7), custom_call_target="tpu_custom_call" | custom-call | tf_op jit(solution)/shard_map/pallas_call | solution.py:256
  26.4 1.9 %collective-permute-start = (s16[16,136,128]{2,1,0:T(8,128)(2,1)S(1)}, s16[16,136,128]{2,1,0:T(8,128)(2,1)S(1)}, u32[]{:S(2)}, u32[]{:S(2)}) collective-permute-start(s16[16,136,128]{2,1,0:T(8,128)(2,1)S(1)} %get-tuple-element.7), channel_id=1, source_target_pairs={{0,8},{8,0},{1,9},{9,1},{2,10},{10,2},{3,11},{11,3},{4,12},{12,4},... | collective-permute-start | bytes 1671176 | tf_op jit(solution)/shard_map/ppermute | solution.py:262
  28.4 1.9 %collective-permute-done.got = s16[16,136,128]{2,1,0:T(8,128)(2,1)S(1)} collective-permute-done((s16[16,136,128]{2,1,0:T(8,128)(2,1)S(1)}, s16[16,136,128]{2,1,0:T(8,128)(2,1)S(1)}, u32[]{:S(2)}, u32[]{:S(2)}) %collective-permute-start) | collective-permute-done | bytes 557088 | tf_op jit(solution)/shard_map/ppermute | solution.py:262
  30.3 0.6 shard_map.70
  30.9 16.3 %all_to_all.16.got = s16[4,4,136,128]{3,2,1,0:T(8,128)(2,1)S(1)} all-to-all(s16[4,4,136,128]{3,2,1,0:T(8,128)(2,1)S(1)} %shard_map.70), channel_id=1, replica_groups=mesh['zq'=8,'z0'=2,'yh'=2,'core'=2,'coef'=8] {'z0','yh'}, dimensions={0} | all-to-all | bytes 1114112 | tf_op jit(solution)/shard_map/all_to_all | solution.py:267
  47.2 0.3 shard_map.71
  47.5 30.0 %all_to_all.17.coded = s16[8,72,128]{2,1,0:T(8,128)(2,1)S(1)} all-to-all(s16[8,72,128]{2,1,0:T(8,128)(2,1)S(1)} %shard_map.71), channel_id=1, replica_groups=mesh['zq'=8,'z0'=2,'yh'=2,'core'=2,'coef'=8] {'zq'}, dimensions={0} | all-to-all | bytes 294912 | tf_op jit(solution)/shard_map/all_to_all | solution.py:269
  77.6 0.8 %shard_map.72 = (f32[128,128]{1,0:T(8,128)}, f32[1,128]{1,0:T(1,128)}) custom-call(s16[8,72,128]{2,1,0:T(8,128)(2,1)S(1)} %all_to_all.17.coded), custom_call_target="tpu_custom_call" | custom-call | tf_op jit(solution)/shard_map/pallas_call | solution.py:270
Async XLA Ops:
  0.6 24.2 %copy-start = (s32[1,32,2]{1,2,0:T(2,128)S(1)}, s32[1,32,2]{1,2,0:T(2,128)}, u32[]{:S(2)}) copy-start(s32[1,32,2]{1,2,0:T(2,128)} %param.6) | copy-start | bytes 772
  26.4 3.9 %collective-permute-start = (s16[16,136,128]{2,1,0:T(8,128)(2,1)S(1)}, s16[16,136,128]{2,1,0:T(8,128)(2,1)S(1)}, u32[]{:S(2)}, u32[]{:S(2)}) collective-permute-start(s16[16,136,128]{2,1,0:T(8,128)(2,1)S(1)} %get-tuple-element.7), channel_id=1, source_target_pairs={{0,8},{8,0},{1,9},{9,1},{2,10},{10,2},{3,11},{11,3},{4,12},{12,4},... | collective-permute-start | bytes 1671176 | tf_op jit(solution)/shard_map/ppermute | solution.py:262

commit v7 on v6

--- a/solution.py
+++ b/solution.py
@@ -18,6 +18,9 @@
 STEPS = 16.0
 TINY = 1e-30
 PER = STEPS / 0.6931471805599453
+
+
+ORDER = [4, 0, 5, 1, 6, 2, 7, 3]
 
 
 def iota(shape, dim):
@@ -185,15 +188,14 @@
     return total
 
 
-def recode_kernel(unroll, got, coded):
-    def body(i):
+def recode_kernel(got, coded):
+    for i in range(got.shape[1]):
         several = [get_two(got, (k, i)) for k in range(got.shape[0])]
         for k in range(2):
             main, tail = encode(*add_up([two[k] for two in several]))
-            coded[2 * i + k, :HALF] = to_int16(main)
-            coded[2 * i + k, HALF:] = to_int16(stack_rows(tail))
-
-    loop(got.shape[1], unroll, body)
+            to = ORDER.index(2 * i + k)
+            coded[to, :HALF] = to_int16(main)
+            coded[to, HALF:] = to_int16(stack_rows(tail))
 
 
 def finish_kernel(coded, diag_out, grad_out):
@@ -265,8 +267,8 @@
         functools.partial(join_kernel, 16), jax.ShapeDtypeStruct((near, far // 2, DUO, BS), i16), "vv"
     )(acc, got)
     landed = lax.all_to_all(coded, ("z0", "yh"), 0, 0, tiled=True)
-    coded = call(functools.partial(recode_kernel, 8), shape(far, i16), "v")(landed)
-    landed = lax.all_to_all(coded, "zq", 0, 0, tiled=True)
+    coded = call(recode_kernel, shape(far, i16), "v")(landed)
+    landed = lax.all_to_all(coded, "zq", 0, 0, tiled=True, axis_index_groups=[ORDER])
     diag, grad = call(
         finish_kernel, [jax.ShapeDtypeStruct((BS, BS), f32), jax.ShapeDtypeStruct((1, BS), f32)], "v"
     )(landed)

time: 79.4 us -> 72.8 us (0.917)
  the two profiles are of different devices: /device:TPU:6 before, /device:TPU:32 now
where the time goes in v7:
time: 72.8 us; the launch traced here: 72.6 us
  blocking collectives  60.7 us (83%)
  Pallas kernels  7.33 us (10%)
  starting transfers between devices  1.92 us (3%)
  waiting for transfers between devices  1.92 us (3%)
    all_to_all x1, blocking collectives, shards(): lax.all_to_all(coded, 'zq', 0, 0, tiled=True, axis_index_groups=[ORDER])  24 us
    all_to_all x1, blocking collectives, shards(): lax.all_to_all(coded, 'coef', 0, 0, tiled=True)  21.7 us
    all_to_all x1, blocking collectives, shards(): landed = lax.all_to_all(coded, ('z0', 'yh'), 0, 0, tiled=True)  15 us
    pallas_call x1, Pallas kernels, shards(): call(functools.partial(products_kernel, 8), jax.ShapeDtypeStruct((groups,...  4.05 us
    ppermute x1, waiting for transfers between devices, shards(): got = lax.ppermute(other, 'core', [(0, 1), (1, 0)])  1.92 us
    ppermute x1, starting transfers between devices, shards(): got = lax.ppermute(other, 'core', [(0, 1), (1, 0)])  1.92 us
    pallas_call x1, Pallas kernels, shards(): call(functools.partial(place_kernel, 16), [shape(slots, f32), jax.ShapeDt...  1.54 us
  transfers between devices with their start and end apart: 1, of which 1 were waited for; matrix products, arithmetic and copies ran while one was open for 0% of the time, Pallas kernels for 0%

profile of v7, /device:TPU:32, one launch (start us, length us, event | category | flops | bytes accessed | tf_op | source)
XLA Modules:
  0.0 72.6 jit_solution(4418121359468530547)
XLA Ops:
  0.6 0.0 copy-start
  0.6 4.1 %shard_map.68 = s16[8,4,136,128]{3,2,1,0:T(8,128)(2,1)S(1)} custom-call(s32[64]{0:T(128)} %runs_hbm.1, bf16[32,128]{1,0:T(8,128)(2,1)} %bitcast.9, f32[32,128]{1,0:T(8,128)} %residual_hbm.1, bf16[4,8,2,128,128]{4,3,2,1,0:T(8,128)(2,1)} %jac_hbm.1), custom_call_target="tpu_custom_call" | custom-call | flops 268435456 | bytes 3145728 | tf_op jit(solution)/shard_map/pallas_call | solution.py:240
  4.7 21.7 %all_to_all.15 = s16[8,4,136,128]{3,2,1,0:T(8,128)(2,1)S(1)} all-to-all(s16[8,4,136,128]{3,2,1,0:T(8,128)(2,1)S(1)} %shard_map.68), channel_id=1, replica_groups=mesh['zq'=8,'z0'=2,'yh'=2,'core'=2,'coef'=8] {'coef'}, dimensions={0} | all-to-all | bytes 2228224 | tf_op jit(solution)/shard_map/all_to_all | solution.py:257
  26.4 0.0 copy-done
  26.4 1.5 %shard_map.69 = (f32[64,72,128]{2,1,0:T(8,128)S(1)}, s16[16,136,128]{2,1,0:T(8,128)(2,1)S(1)}) custom-call(s32[2,32]{1,0:T(2,128)S(1)} %bitcast.8, s16[32,136,128]{2,1,0:T(8,128)(2,1)S(1)} %bitcast.7), custom_call_target="tpu_custom_call" | custom-call | tf_op jit(solution)/shard_map/pallas_call | solution.py:258
  28.0 1.9 %collective-permute-start = (s16[16,136,128]{2,1,0:T(8,128)(2,1)S(1)}, s16[16,136,128]{2,1,0:T(8,128)(2,1)S(1)}, u32[]{:S(2)}, u32[]{:S(2)}) collective-permute-start(s16[16,136,128]{2,1,0:T(8,128)(2,1)S(1)} %get-tuple-element.7), channel_id=1, source_target_pairs={{0,8},{8,0},{1,9},{9,1},{2,10},{10,2},{3,11},{11,3},{4,12},{12,4},... | collective-permute-start | bytes 1671176 | tf_op jit(solution)/shard_map/ppermute | solution.py:264
  29.9 1.9 %collective-permute-done.got = s16[16,136,128]{2,1,0:T(8,128)(2,1)S(1)} collective-permute-done((s16[16,136,128]{2,1,0:T(8,128)(2,1)S(1)}, s16[16,136,128]{2,1,0:T(8,128)(2,1)S(1)}, u32[]{:S(2)}, u32[]{:S(2)}) %collective-permute-start) | collective-permute-done | bytes 557088 | tf_op jit(solution)/shard_map/ppermute | solution.py:264
  31.8 0.6 shard_map.70
  32.4 15.0 %all_to_all.16.got = s16[4,4,136,128]{3,2,1,0:T(8,128)(2,1)S(1)} all-to-all(s16[4,4,136,128]{3,2,1,0:T(8,128)(2,1)S(1)} %shard_map.70), channel_id=1, replica_groups=mesh['zq'=8,'z0'=2,'yh'=2,'core'=2,'coef'=8] {'z0','yh'}, dimensions={0} | all-to-all | bytes 1114112 | tf_op jit(solution)/shard_map/all_to_all | solution.py:269
  47.4 0.3 shard_map.71
  47.8 24.0 %all_to_all.17.coded = s16[8,72,128]{2,1,0:T(8,128)(2,1)S(1)} all-to-all(s16[8,72,128]{2,1,0:T(8,128)(2,1)S(1)} %shard_map.71), channel_id=1, replica_groups={{256,0,320,64,384,128,448,192},{257,1,321,65,385,129,449,193},{258,2,32..., dimensions={0} | all-to-all | bytes 294912 | tf_op jit(solution)/shard_map/all_to_all | solution.py:271
  71.8 0.8 %shard_map.72 = (f32[128,128]{1,0:T(8,128)}, f32[1,128]{1,0:T(1,128)}) custom-call(s16[8,72,128]{2,1,0:T(8,128)(2,1)S(1)} %all_to_all.17.coded), custom_call_target="tpu_custom_call" | custom-call | tf_op jit(solution)/shard_map/pallas_call | solution.py:272
Async XLA Ops:
  0.6 25.8 %copy-start = (s32[1,32,2]{1,2,0:T(2,128)S(1)}, s32[1,32,2]{1,2,0:T(2,128)}, u32[]{:S(2)}) copy-start(s32[1,32,2]{1,2,0:T(2,128)} %param.6) | copy-start | bytes 772
  28.0 3.9 %collective-permute-start = (s16[16,136,128]{2,1,0:T(8,128)(2,1)S(1)}, s16[16,136,128]{2,1,0:T(8,128)(2,1)S(1)}, u32[]{:S(2)}, u32[]{:S(2)}) collective-permute-start(s16[16,136,128]{2,1,0:T(8,128)(2,1)S(1)} %get-tuple-element.7), channel_id=1, source_target_pairs={{0,8},{8,0},{1,9},{9,1},{2,10},{10,2},{3,11},{11,3},{4,12},{12,4},... | collective-permute-start | bytes 1671176 | tf_op jit(solution)/shard_map/ppermute | solution.py:264

commit v8 on v7

--- a/solution.py
+++ b/solution.py
@@ -20,7 +20,10 @@
 PER = STEPS / 0.6931471805599453
 
 
-ORDER = [4, 0, 5, 1, 6, 2, 7, 3]
+ORDER = [4, 0, 6, 2, 5, 1, 7, 3]
+
+
+FLIP = 7
 
 
 def iota(shape, dim):
@@ -133,7 +136,7 @@
                 diag = jnp.sum(jnp.where(lanes, last, 0.0), axis=0, keepdims=True)
                 grad = jnp.sum(out[BS : BS + 8], axis=0, keepdims=True)
                 two.append(encode(packed, diag, grad))
-            put_two(coded, (g, r), two)
+            put_two(coded, (lax.bitwise_xor(g, FLIP), r), two)
 
         loop(groups, unroll, body)
 
@@ -144,9 +147,12 @@
     acc[...] = jnp.zeros_like(acc)
     copy.wait()
 
+    rows = coded.shape[0] // lax.axis_size("coef")
+
     def body(row):
+        source = lax.bitwise_xor(lax.div(row, rows), FLIP)
         for s, (packed, diag, grad) in enumerate(get_two(coded, (row,))):
-            where = targets[s, row]
+            where = targets[s, source * rows + lax.rem(row, rows)]
             acc[where, :HALF] += packed
             acc[where, HALF:] += stack_rows([diag, grad])
 
@@ -254,7 +260,7 @@
         flops=2 * n_items * BS**3,
         moved=n_items * BS * BS * 3,
     )(*[pltpu.with_memory_space_constraint(x, pltpu.HBM) for x in (run_of_half, run_scale.reshape(-1, BS), residual, jac_blocks)])
-    landed = lax.all_to_all(coded, "coef", 0, 0, tiled=True).reshape(n_items // PAIR, DUO, BS)
+    landed = lax.all_to_all(coded, "coef", 0, 0, tiled=True, axis_index_groups=[[g ^ FLIP for g in range(groups)]]).reshape(n_items // PAIR, DUO, BS)
     acc, other = call(
         functools.partial(place_kernel, 16),
         [shape(slots, f32), jax.ShapeDtypeStruct((slots // 4, DUO, BS), i16)],

time: 72.8 us -> 71.1 us (0.977)
  the two profiles are of different devices: /device:TPU:32 before, /device:TPU:6 now
where the time goes in v8:
time: 71.1 us; the launch traced here: 70.7 us
  blocking collectives  58.9 us (83%)
  Pallas kernels  7.33 us (10%)
  starting transfers between devices  1.92 us (3%)
  waiting for transfers between devices  1.92 us (3%)
    all_to_all x1, blocking collectives, shards(): lax.all_to_all(coded, 'zq', 0, 0, tiled=True, axis_index_groups=[ORDER])  23.2 us
    all_to_all x1, blocking collectives, shards(): lax.all_to_all(coded, 'coef', 0, 0, tiled=True, axis_index_groups=[[g ^ F...  19.3 us
    all_to_all x1, blocking collectives, shards(): landed = lax.all_to_all(coded, ('z0', 'yh'), 0, 0, tiled=True)  16.4 us
    pallas_call x1, Pallas kernels, shards(): call(functools.partial(products_kernel, 8), jax.ShapeDtypeStruct((groups,...  4.05 us
    ppermute x1, waiting for transfers between devices, shards(): got = lax.ppermute(other, 'core', [(0, 1), (1, 0)])  1.92 us
    ppermute x1, starting transfers between devices, shards(): got = lax.ppermute(other, 'core', [(0, 1), (1, 0)])  1.92 us
    pallas_call x1, Pallas kernels, shards(): call(functools.partial(place_kernel, 16), [shape(slots, f32), jax.ShapeDt...  1.55 us
  transfers between devices with their start and end apart: 1, of which 1 were waited for; matrix products, arithmetic and copies ran while one was open for 0% of the time, Pallas kernels for 0%

profile of v8, /device:TPU:6, one launch (start us, length us, event | category | flops | bytes accessed | tf_op | source)
XLA Modules:
  0.0 70.7 jit_solution(174729030174258412)
XLA Ops:
  0.6 0.0 copy-start
  0.6 4.0 %shard_map.68 = s16[8,4,136,128]{3,2,1,0:T(8,128)(2,1)S(1)} custom-call(s32[64]{0:T(128)} %runs_hbm.1, bf16[32,128]{1,0:T(8,128)(2,1)} %bitcast.9, f32[32,128]{1,0:T(8,128)} %residual_hbm.1, bf16[4,8,2,128,128]{4,3,2,1,0:T(8,128)(2,1)} %jac_hbm.1), custom_call_target="tpu_custom_call" | custom-call | flops 268435456 | bytes 3145728 | tf_op jit(solution)/shard_map/pallas_call | solution.py:246
  4.7 19.3 %all_to_all.15 = s16[8,4,136,128]{3,2,1,0:T(8,128)(2,1)S(1)} all-to-all(s16[8,4,136,128]{3,2,1,0:T(8,128)(2,1)S(1)} %shard_map.68), channel_id=1, replica_groups={{7,6,5,4,3,2,1,0},{15,14,13,12,11,10,9,8},{23,22,21,20,19,18,17,16},{31..., dimensions={0} | all-to-all | bytes 2228224 | tf_op jit(solution)/shard_map/all_to_all | solution.py:263
  24.0 0.0 copy-done
  24.0 1.5 %shard_map.69 = (f32[64,72,128]{2,1,0:T(8,128)S(1)}, s16[16,136,128]{2,1,0:T(8,128)(2,1)S(1)}) custom-call(s32[2,32]{1,0:T(2,128)S(1)} %bitcast.8, s16[32,136,128]{2,1,0:T(8,128)(2,1)S(1)} %bitcast.7), custom_call_target="tpu_custom_call" | custom-call | tf_op jit(solution)/shard_map/pallas_call | solution.py:264
  25.6 1.9 %collective-permute-start = (s16[16,136,128]{2,1,0:T(8,128)(2,1)S(1)}, s16[16,136,128]{2,1,0:T(8,128)(2,1)S(1)}, u32[]{:S(2)}, u32[]{:S(2)}) collective-permute-start(s16[16,136,128]{2,1,0:T(8,128)(2,1)S(1)} %get-tuple-element.7), channel_id=1, source_target_pairs={{0,8},{8,0},{1,9},{9,1},{2,10},{10,2},{3,11},{11,3},{4,12},{12,4},... | collective-permute-start | bytes 1671176 | tf_op jit(solution)/shard_map/ppermute | solution.py:270
  27.5 1.9 %collective-permute-done.got = s16[16,136,128]{2,1,0:T(8,128)(2,1)S(1)} collective-permute-done((s16[16,136,128]{2,1,0:T(8,128)(2,1)S(1)}, s16[16,136,128]{2,1,0:T(8,128)(2,1)S(1)}, u32[]{:S(2)}, u32[]{:S(2)}) %collective-permute-start) | collective-permute-done | bytes 557088 | tf_op jit(solution)/shard_map/ppermute | solution.py:270
  29.4 0.6 shard_map.70
  30.0 16.4 %all_to_all.16.got = s16[4,4,136,128]{3,2,1,0:T(8,128)(2,1)S(1)} all-to-all(s16[4,4,136,128]{3,2,1,0:T(8,128)(2,1)S(1)} %shard_map.70), channel_id=1, replica_groups=mesh['zq'=8,'z0'=2,'yh'=2,'core'=2,'coef'=8] {'z0','yh'}, dimensions={0} | all-to-all | bytes 1114112 | tf_op jit(solution)/shard_map/all_to_all | solution.py:275
  46.4 0.3 shard_map.71
  46.7 23.2 %all_to_all.17.coded = s16[8,72,128]{2,1,0:T(8,128)(2,1)S(1)} all-to-all(s16[8,72,128]{2,1,0:T(8,128)(2,1)S(1)} %shard_map.71), channel_id=1, replica_groups={{256,0,384,128,320,64,448,192},{257,1,385,129,321,65,449,193},{258,2,38..., dimensions={0} | all-to-all | bytes 294912 | tf_op jit(solution)/shard_map/all_to_all | solution.py:277
  69.9 0.8 %shard_map.72 = (f32[128,128]{1,0:T(8,128)}, f32[1,128]{1,0:T(1,128)}) custom-call(s16[8,72,128]{2,1,0:T(8,128)(2,1)S(1)} %all_to_all.17.coded), custom_call_target="tpu_custom_call" | custom-call | tf_op jit(solution)/shard_map/pallas_call | solution.py:278
Async XLA Ops:
  0.6 23.4 %copy-start = (s32[1,32,2]{1,2,0:T(2,128)S(1)}, s32[1,32,2]{1,2,0:T(2,128)}, u32[]{:S(2)}) copy-start(s32[1,32,2]{1,2,0:T(2,128)} %param.6) | copy-start | bytes 772
  25.6 3.9 %collective-permute-start = (s16[16,136,128]{2,1,0:T(8,128)(2,1)S(1)}, s16[16,136,128]{2,1,0:T(8,128)(2,1)S(1)}, u32[]{:S(2)}, u32[]{:S(2)}) collective-permute-start(s16[16,136,128]{2,1,0:T(8,128)(2,1)S(1)} %get-tuple-element.7), channel_id=1, source_target_pairs={{0,8},{8,0},{1,9},{9,1},{2,10},{10,2},{3,11},{11,3},{4,12},{12,4},... | collective-permute-start | bytes 1671176 | tf_op jit(solution)/shard_map/ppermute | solution.py:270

commit v9 on v8

--- a/solution.py
+++ b/solution.py
@@ -182,7 +182,7 @@
                 parts = mine[:HALF], mine[HALF : HALF + 1], mine[HALF + 1 : HALF + 2]
                 new[y].append(encode(*[p + q for p, q in zip(parts, more)]))
         for y in range(2):
-            put_two(coded, (2 * bit + y, far), new[y])
+            put_two(coded, (3 - 2 * bit - y, far), new[y])
 
     loop(got.shape[0] // 2, unroll, body)
 
@@ -272,7 +272,7 @@
     coded = call(
         functools.partial(join_kernel, 16), jax.ShapeDtypeStruct((near, far // 2, DUO, BS), i16), "vv"
     )(acc, got)
-    landed = lax.all_to_all(coded, ("z0", "yh"), 0, 0, tiled=True)
+    landed = lax.all_to_all(coded, "zy", 0, 0, tiled=True, axis_index_groups=[[i ^ 3 for i in range(4)]])
     coded = call(recode_kernel, shape(far, i16), "v")(landed)
     landed = lax.all_to_all(coded, "zq", 0, 0, tiled=True, axis_index_groups=[ORDER])
     diag, grad = call(
@@ -282,8 +282,8 @@
 
 
 def solution(mesh):
-    fine = Mesh(mesh.devices.reshape(-1, 2, 2, 2, mesh.devices.shape[1]), ("zq", "z0", "yh", "core", "coef"))
-    batch = ("zq", "z0", "yh", "core")
+    fine = Mesh(mesh.devices.reshape(-1, 4, 2, mesh.devices.shape[1]), ("zq", "zy", "core", "coef"))
+    batch = ("zq", "zy", "core")
     in_specs = (
         P(batch + ("coef",), None, None, None, None),
         P("coef", batch, None),

time: 71.1 us -> 70.5 us (level)
  the two profiles are of different devices: /device:TPU:6 before, /device:TPU:24 now
where the time goes in v9:
time: 70.5 us; the launch traced here: 70.2 us
  blocking collectives  58.4 us (83%)
  Pallas kernels  7.33 us (10%)
  starting transfers between devices  1.92 us (3%)
  waiting for transfers between devices  1.92 us (3%)
    all_to_all x1, blocking collectives, shards(): lax.all_to_all(coded, 'zq', 0, 0, tiled=True, axis_index_groups=[ORDER])  24.2 us
    all_to_all x1, blocking collectives, shards(): lax.all_to_all(coded, 'coef', 0, 0, tiled=True, axis_index_groups=[[g ^ F...  20.1 us
    all_to_all x1, blocking collectives, shards(): lax.all_to_all(coded, 'zy', 0, 0, tiled=True, axis_index_groups=[[i ^ 3 f...  14.1 us
    pallas_call x1, Pallas kernels, shards(): call(functools.partial(products_kernel, 8), jax.ShapeDtypeStruct((groups,...  4.05 us
    ppermute x1, waiting for transfers between devices, shards(): got = lax.ppermute(other, 'core', [(0, 1), (1, 0)])  1.92 us
    ppermute x1, starting transfers between devices, shards(): got = lax.ppermute(other, 'core', [(0, 1), (1, 0)])  1.92 us
    pallas_call x1, Pallas kernels, shards(): call(functools.partial(place_kernel, 16), [shape(slots, f32), jax.ShapeDt...  1.55 us
  transfers between devices with their start and end apart: 1, of which 1 were waited for; matrix products, arithmetic and copies ran while one was open for 0% of the time, Pallas kernels for 0%

profile of v9, /device:TPU:24, one launch (start us, length us, event | category | flops | bytes accessed | tf_op | source)
XLA Modules:
  0.0 70.2 jit_solution(5674039155213085141)
XLA Ops:
  0.6 0.0 copy-start
  0.6 4.0 %shard_map.68 = s16[8,4,136,128]{3,2,1,0:T(8,128)(2,1)S(1)} custom-call(s32[64]{0:T(128)} %runs_hbm.1, bf16[32,128]{1,0:T(8,128)(2,1)} %bitcast.9, f32[32,128]{1,0:T(8,128)} %residual_hbm.1, bf16[4,8,2,128,128]{4,3,2,1,0:T(8,128)(2,1)} %jac_hbm.1), custom_call_target="tpu_custom_call" | custom-call | flops 268435456 | bytes 3145728 | tf_op jit(solution)/shard_map/pallas_call | solution.py:246
  4.7 20.1 %all_to_all.15 = s16[8,4,136,128]{3,2,1,0:T(8,128)(2,1)S(1)} all-to-all(s16[8,4,136,128]{3,2,1,0:T(8,128)(2,1)S(1)} %shard_map.68), channel_id=1, replica_groups={{7,6,5,4,3,2,1,0},{15,14,13,12,11,10,9,8},{23,22,21,20,19,18,17,16},{31..., dimensions={0} | all-to-all | bytes 2228224 | tf_op jit(solution)/shard_map/all_to_all | solution.py:263
  24.8 0.0 copy-done
  24.8 1.5 %shard_map.69 = (f32[64,72,128]{2,1,0:T(8,128)S(1)}, s16[16,136,128]{2,1,0:T(8,128)(2,1)S(1)}) custom-call(s32[2,32]{1,0:T(2,128)S(1)} %bitcast.8, s16[32,136,128]{2,1,0:T(8,128)(2,1)S(1)} %bitcast.7), custom_call_target="tpu_custom_call" | custom-call | tf_op jit(solution)/shard_map/pallas_call | solution.py:264
  26.3 1.9 %collective-permute-start = (s16[16,136,128]{2,1,0:T(8,128)(2,1)S(1)}, s16[16,136,128]{2,1,0:T(8,128)(2,1)S(1)}, u32[]{:S(2)}, u32[]{:S(2)}) collective-permute-start(s16[16,136,128]{2,1,0:T(8,128)(2,1)S(1)} %get-tuple-element.7), channel_id=1, source_target_pairs={{0,8},{8,0},{1,9},{9,1},{2,10},{10,2},{3,11},{11,3},{4,12},{12,4},... | collective-permute-start | bytes 1671176 | tf_op jit(solution)/shard_map/ppermute | solution.py:270
  28.3 1.9 %collective-permute-done.got = s16[16,136,128]{2,1,0:T(8,128)(2,1)S(1)} collective-permute-done((s16[16,136,128]{2,1,0:T(8,128)(2,1)S(1)}, s16[16,136,128]{2,1,0:T(8,128)(2,1)S(1)}, u32[]{:S(2)}, u32[]{:S(2)}) %collective-permute-start) | collective-permute-done | bytes 557088 | tf_op jit(solution)/shard_map/ppermute | solution.py:270
  30.2 0.6 shard_map.70
  30.8 14.1 %all_to_all.16.got = s16[4,4,136,128]{3,2,1,0:T(8,128)(2,1)S(1)} all-to-all(s16[4,4,136,128]{3,2,1,0:T(8,128)(2,1)S(1)} %shard_map.70), channel_id=1, replica_groups={{48,32,16,0},{49,33,17,1},{50,34,18,2},{51,35,19,3},{52,36,20,4},{53,37..., dimensions={0} | all-to-all | bytes 1114112 | tf_op jit(solution)/shard_map/all_to_all | solution.py:275
  44.9 0.3 shard_map.71
  45.2 24.2 %all_to_all.17.coded = s16[8,72,128]{2,1,0:T(8,128)(2,1)S(1)} all-to-all(s16[8,72,128]{2,1,0:T(8,128)(2,1)S(1)} %shard_map.71), channel_id=1, replica_groups={{256,0,384,128,320,64,448,192},{257,1,385,129,321,65,449,193},{258,2,38..., dimensions={0} | all-to-all | bytes 294912 | tf_op jit(solution)/shard_map/all_to_all | solution.py:277
  69.4 0.8 %shard_map.72 = (f32[128,128]{1,0:T(8,128)}, f32[1,128]{1,0:T(1,128)}) custom-call(s16[8,72,128]{2,1,0:T(8,128)(2,1)S(1)} %all_to_all.17.coded), custom_call_target="tpu_custom_call" | custom-call | tf_op jit(solution)/shard_map/pallas_call | solution.py:278
Async XLA Ops:
  0.6 24.1 %copy-start = (s32[1,32,2]{1,2,0:T(2,128)S(1)}, s32[1,32,2]{1,2,0:T(2,128)}, u32[]{:S(2)}) copy-start(s32[1,32,2]{1,2,0:T(2,128)} %param.6) | copy-start | bytes 772
  26.3 3.9 %collective-permute-start = (s16[16,136,128]{2,1,0:T(8,128)(2,1)S(1)}, s16[16,136,128]{2,1,0:T(8,128)(2,1)S(1)}, u32[]{:S(2)}, u32[]{:S(2)}) collective-permute-start(s16[16,136,128]{2,1,0:T(8,128)(2,1)S(1)} %get-tuple-element.7), channel_id=1, source_target_pairs={{0,8},{8,0},{1,9},{9,1},{2,10},{10,2},{3,11},{11,3},{4,12},{12,4},... | collective-permute-start | bytes 1671176 | tf_op jit(solution)/shard_map/ppermute | solution.py:270
